TPU v7x, 32 devices: a whole 2x2x4 slice. The times are simulated.
32 devices in a mesh: seq: 8 (over z, y), dp: 4 (over x, core).
Axes of the slice: x: 2, y: 2, z: 4, core: 2. Of those that a mesh axis runs over, the one named last changes fastest.
Arguments:
- gate_in: bfloat16 [4, 2048, 1024], P('dp', None, 'seq'), may hold values from -6 to 6
- values_in: bfloat16 [4, 2048, 1024], P('dp', None, 'seq'), may hold values from -6 to 6
- out_grad: bfloat16 [4, 2048, 1024], P('dp', None, 'seq'), may hold values from -0.1875 to 0.1875
- filter_taps: float32 [2048, 1024], P(None, 'seq'), may hold values from -6 to 6
Outputs:
- grad_gate: bfloat16 [4, 2048, 1024], P('dp', None, 'seq')
- grad_values: bfloat16 [4, 2048, 1024], P('dp', None, 'seq')
- grad_filter: float32 [2048, 1024], P('dp', 'seq')
All inputs are finite; a program needn't handle non-finite values.
Results may differ from a plain program's by a relative error of at most 0.005.
Values may be sent and summed in bfloat16 or wider, within the bound.
No kernel may reach another device: no remote copies, remote signals or barrier semaphores. Data moves between devices by JAX's collectives and lax.ppermute only.
A program may use at most 128 MiB of HBM per device.

v0:
```python
import math

import jax
import jax.numpy as jnp
from jax import lax
from jax.sharding import PartitionSpec as P

precise = lax.Precision.HIGHEST
coarse = lax.Precision.HIGH


def spin_tables(count_in, count_out, period):
    rows = lax.broadcasted_iota(jnp.int32, (count_in, count_out), 0)
    cols = lax.broadcasted_iota(jnp.int32, (count_in, count_out), 1)
    phase = (rows * cols % period).astype(jnp.float32) * (2.0 * math.pi / period)
    return (jnp.cos(phase), jnp.sin(phase))


def make_tables(length, columns):
    rows_in = length // columns
    rows_out = 2 * rows_in
    first_cos, first_sin = spin_tables(rows_in, rows_out, rows_out)
    turn = spin_tables(rows_out, columns, 2 * length)
    last_cos, last_sin = spin_tables(columns, columns, columns)
    first_fwd = jnp.concatenate([first_cos, -first_sin], axis=1)
    last_fwd = jnp.concatenate(
        [
            jnp.concatenate([last_cos, -last_sin], axis=1),
            jnp.concatenate([last_sin, last_cos], axis=1),
        ],
        axis=0,
    )
    last_inv = jnp.concatenate(
        [
            jnp.concatenate([last_cos.T, last_sin.T], axis=1),
            jnp.concatenate([-last_sin.T, last_cos.T], axis=1),
        ],
        axis=0,
    )
    first_inv = jnp.concatenate(
        [
            jnp.concatenate([first_cos.T, first_sin.T], axis=1),
            jnp.concatenate([-first_sin.T, first_cos.T], axis=1),
        ],
        axis=0,
    )
    return (first_fwd, turn, last_fwd, last_inv, first_inv)


def spectrum(signal, tables, columns, first_precision):
    first_fwd, (turn_cos, turn_sin), last_fwd, last_inv, first_inv = tables
    held, length = signal.shape
    half = turn_cos.shape[0]
    grid = signal.reshape(held, length // columns, columns)
    part = jnp.einsum("cmn,mk->ckn", grid, first_fwd, precision=first_precision)
    part_real = part[:, :half]
    part_imag = part[:, half:]
    turned = jnp.concatenate(
        [part_real * turn_cos + part_imag * turn_sin, part_imag * turn_cos - part_real * turn_sin],
        axis=2,
    )
    out = jnp.einsum("ckn,nj->ckj", turned, last_fwd, precision=first_precision)
    return (out[:, :, :columns], out[:, :, columns:])


def to_signal(spec_real, spec_imag, tables, length):
    first_fwd, (turn_cos, turn_sin), last_fwd, last_inv, first_inv = tables
    held = spec_real.shape[0]
    columns = spec_real.shape[2]
    rows_in = length // columns
    stacked = jnp.concatenate([spec_real, spec_imag], axis=2)
    back = jnp.einsum("ckj,jn->ckn", stacked, last_inv, precision=coarse)
    back_real = back[:, :, :columns]
    back_imag = back[:, :, columns:]
    turned = jnp.concatenate(
        [back_real * turn_cos - back_imag * turn_sin, back_imag * turn_cos + back_real * turn_sin],
        axis=1,
    )
    factor = 1.0 / (2 * length)
    both = jnp.einsum("ckn,km->cmn", turned, first_inv, precision=coarse) * factor
    real_part = both[:, :rows_in]
    imag_part = both[:, rows_in:]
    return (real_part.reshape(held, length), imag_part.reshape(held, length))


def shards(gate_in, values_in, out_grad, filter_taps):
    seq_count = lax.axis_size("seq")
    group_count = lax.axis_size("dp")
    channels = gate_in.shape[1]
    shard_len = gate_in.shape[2]
    length = shard_len * seq_count
    quarter = channels // group_count
    per_block = quarter // seq_count
    held_channels = group_count * per_block
    columns = 128 if length % 128 == 0 and length >= 8192 else 32
    tables = make_tables(length, columns)
    gate_wide = gate_in[0].astype(jnp.float32)
    values_wide = values_in[0].astype(jnp.float32)
    mixed = (gate_wide * values_wide).astype(jnp.bfloat16)
    grad_rows, mixed_rows = (
        lax.all_to_all(
            out_grad[0].reshape(group_count, quarter, shard_len),
            "seq",
            split_axis=1,
            concat_axis=2,
            tiled=True,
        ),
        lax.all_to_all(
            mixed.reshape(group_count, quarter, shard_len),
            "seq",
            split_axis=1,
            concat_axis=2,
            tiled=True,
        ),
    )
    filter_grouped = filter_taps.reshape(group_count, quarter, shard_len)
    filter_rows = lax.all_to_all(filter_grouped, "seq", split_axis=1, concat_axis=2, tiled=True)
    grad_real, grad_imag = spectrum(
        grad_rows.reshape(held_channels, length).astype(jnp.float32), tables, columns, coarse
    )
    mix_real, mix_imag = spectrum(
        mixed_rows.reshape(held_channels, length).astype(jnp.float32), tables, columns, coarse
    )
    tap_real, tap_imag = spectrum(
        filter_rows.reshape(held_channels, length), tables, columns, precise
    )
    carry_real = tap_real * grad_real + tap_imag * grad_imag
    carry_imag = tap_real * grad_imag - tap_imag * grad_real
    lag_real = grad_real * mix_real + grad_imag * mix_imag
    lag_imag = grad_imag * mix_real - grad_real * mix_imag
    carried, lagged = to_signal(carry_real - lag_imag, carry_imag + lag_real, tables, length)
    carried = carried.astype(jnp.bfloat16).reshape(group_count, per_block, length)
    returned = lax.all_to_all(carried, "seq", split_axis=2, concat_axis=1, tiled=True)
    carried_home = returned.reshape(channels, shard_len).astype(jnp.float32)
    lagged = lagged.reshape(group_count, per_block, length)
    summed = lax.psum_scatter(lagged, "dp", scatter_dimension=0, tiled=True)
    grad_filter = lax.all_to_all(summed, "seq", split_axis=2, concat_axis=1, tiled=True).reshape(
        quarter, shard_len
    )
    grad_gate = (carried_home * values_wide).astype(jnp.bfloat16)[None]
    grad_values = (carried_home * gate_wide).astype(jnp.bfloat16)[None]
    return (grad_gate, grad_values, grad_filter)


def solution(mesh):
    return jax.shard_map(
        shards,
        mesh=mesh,
        in_specs=(P("dp", None, "seq"), P("dp", None, "seq"), P("dp", None, "seq"), P(None, "seq")),
        out_specs=(P("dp", None, "seq"), P("dp", None, "seq"), P("dp", "seq")),
        check_vma=False,
    )
```

profile of v0, /device:TPU:0, one launch (start us, length us, event | category | flops | bytes accessed | tf_op | source)
XLA Modules:
  0.0 172.7 jit_solution(3533968364329271182)
XLA Ops:
  9.8 7.3 %all-to-all-start.2 = ((bf16[4,512,128]{2,0,1:T(4,128)(2,1)}), bf16[4,512,128]{2,0,1:T(4,128)(2,1)S(1)}, u32[]{:S(2)}, u32[]{:S(2)}) async-start(bf16[4,512,128]{2,0,1:T(4,128)(2,1)} %copy.152), calls=%async_computation.2 | async-start | bytes 1048576 | tf_op jit(solution)/shard_map/all_to_all | solution.py:108
  18.3 13.3 %all-to-all-done.2 = bf16[4,512,128]{2,0,1:T(4,128)(2,1)S(1)} async-done(((bf16[4,512,128]{2,0,1:T(4,128)(2,1)}), bf16[4,512,128]{2,0,1:T(4,128)(2,1)S(1)}, u32[]{:S(2)}, u32[]{:S(2)}) %all-to-all-start.2) | async-done | bytes 524320 | tf_op jit(solution)/shard_map/all_to_all | solution.py:108
  31.6 3.6 %all-to-all-start.1 = ((bf16[4,512,128]{2,0,1:T(4,128)(2,1)}), bf16[4,512,128]{2,0,1:T(4,128)(2,1)S(1)}, u32[]{:S(2)}, u32[]{:S(2)}) async-start(bf16[4,512,128]{2,0,1:T(4,128)(2,1)} %copy.147), calls=%async_computation.1 | async-start | bytes 1048576 | tf_op jit(solution)/shard_map/all_to_all | solution.py:101
  35.2 1.7 copy.142
  36.9 12.9 %all-to-all-done.1 = bf16[4,512,128]{2,0,1:T(4,128)(2,1)S(1)} async-done(((bf16[4,512,128]{2,0,1:T(4,128)(2,1)}), bf16[4,512,128]{2,0,1:T(4,128)(2,1)S(1)}, u32[]{:S(2)}, u32[]{:S(2)}) %all-to-all-start.1) | async-done | bytes 524320 | tf_op jit(solution)/shard_map/all_to_all | solution.py:101
  49.9 3.6 %all-to-all-start = ((f32[4,512,128]{2,0,1:T(4,128)}), f32[4,512,128]{2,0,1:T(4,128)S(1)}, u32[]{:S(2)}, u32[]{:S(2)}) async-start(f32[4,512,128]{2,0,1:T(4,128)} %copy.142), calls=%async_computation | async-start | bytes 2097152 | tf_op jit(solution)/shard_map/all_to_all | solution.py:117
  58.2 3.4 %convolution_bitcast_fusion = f32[256,128,32]{0,1,2:T(8,128)} fusion(bf16[256,32,32]{0,2,1:T(8,128)(2,1)S(1)} %reshape.82, f32[32,64]{1,0:T(8,128)S(1)} %get-tuple-element.21, f32[32,64]{1,0:T(8,128)S(1)} %get-tuple-element.22), kind=kOutput, calls=%fused_computation.17 | convolution fusion | flops 201330688 | bytes 4734976 | tf_op jit(solution)/shard_map/cmn,mk->ckn/dot_general | solution.py:55
  61.6 3.3 %convolution_bitcast_fusion.1 = f32[256,128,32]{0,1,2:T(8,128)} fusion(bf16[256,32,32]{0,2,1:T(8,128)(2,1)S(1)} %reshape.81, f32[32,64]{1,0:T(8,128)S(1)} %get-tuple-element.21, f32[32,64]{1,0:T(8,128)S(1)} %get-tuple-element.22), kind=kOutput, calls=%fused_computation.18 | convolution fusion | flops 201330688 | bytes 4734976 | tf_op jit(solution)/shard_map/cmn,mk->ckn/dot_general | solution.py:55
  64.9 14.6 %all-to-all-done = f32[4,512,128]{2,0,1:T(4,128)S(1)} async-done(((f32[4,512,128]{2,0,1:T(4,128)}), f32[4,512,128]{2,0,1:T(4,128)S(1)}, u32[]{:S(2)}, u32[]{:S(2)}) %all-to-all-start) | async-done | bytes 1048608 | tf_op jit(solution)/shard_map/all_to_all | solution.py:117
  81.6 3.7 %convolution_bitcast_fusion.2 = f32[256,128,32]{0,1,2:T(8,128)S(1)} fusion(f32[256,32,32]{0,2,1:T(8,128)S(1)} %reshape_reshape.6, f32[32,64]{1,0:T(8,128)S(1)} %get-tuple-element.21, f32[32,64]{1,0:T(8,128)S(1)} %get-tuple-element.22), kind=kOutput, calls=%fused_computation.19 | convolution fusion | flops 402657280 | bytes 5259264 | tf_op jit(solution)/shard_map/cmn,mk->ckn/dot_general | solution.py:55
  85.3 3.6 %multiply_add_fusion.3 = (f32[256,64,32]{0,1,2:T(8,128)S(1)}, f32[256,64,32]{0,1,2:T(8,128)S(1)}, f32[256,64,32]{0,1,2:T(8,128)S(1)}, f32[256,64,32]{0,1,2:T(8,1...) fusion(f32[256,128,32]{0,1,2:T(8,128)S(1)} %convolution_bitcast_fusion.2, ...), kind=kLoop, calls=%fused_computation.30 | loop fusion | flops 9437184 | bytes 25182208 | tf_op jit(solution)/shard_map/add | solution.py:59
  90.0 6.7 %fusion.12 = f32[256,64,64]{0,2,1:T(8,128)S(1)} fusion(f32[256,64,64]{0,1,2:T(8,128)S(1)} %pad_maximum_fusion, f32[32,32]{0,1:T(8,128)S(1)} %get-tuple-element.26, f32[32,32]{0,1:T(8,128)S(1)} %get-tuple-element.25, f32[32,32]{0,1:T(8,128)S(1)} %fusion.66), kind=kOutput, calls=%fused_computation.15 | convolution fusion | flops 805318656 | bytes 8400896 | tf_op jit(solution)/shard_map/ckn,nj->ckj/dot_general | solution.py:62
  96.6 4.3 %fusion.10 = f32[256,64,64]{0,2,1:T(8,128)S(1)} fusion(f32[256,64,64]{0,1,2:T(8,128)S(1)} %pad_maximum_fusion.1, f32[32,32]{0,1:T(8,128)S(1)} %get-tuple-element.26, f32[32,32]{0,1:T(8,128)S(1)} %get-tuple-element.25, f32[32,32]{0,1:T(8,128)S(1)} %fusion.66), kind=kOutput, calls=%fused_computation.13 | convolution fusion | flops 402665472 | bytes 8400896 | tf_op jit(solution)/shard_map/ckn,nj->ckj/dot_general | solution.py:62
  101.4 4.7 %fusion.8 = f32[256,64,64]{0,2,1:T(8,128)S(1)} fusion(f32[256,64,64]{0,1,2:T(8,128)S(1)} %pad_maximum_fusion.2, f32[32,32]{0,1:T(8,128)S(1)} %get-tuple-element.26, f32[32,32]{0,1:T(8,128)S(1)} %get-tuple-element.25, f32[32,32]{0,1:T(8,128)S(1)} %fusion.66), kind=kOutput, calls=%fused_computation.11 | convolution fusion | flops 402665472 | bytes 8400896 | tf_op jit(solution)/shard_map/ckn,nj->ckj/dot_general | solution.py:62
  106.1 2.0 %subtract_subtract_fusion = (f32[256,64,32]{0,2,1:T(8,128)S(1)}, f32[256,64,32]{0,2,1:T(8,128)S(1)}) fusion(f32[256,64,64]{0,2,1:T(8,128)S(1)} %fusion.8, f32[256,64,64]{0,2,1:T(8,128)S(1)} %fusion.10, f32[256,64,64]{0,2,1:T(8,128)S(1)} %fusion.12), kind=kLoop, calls=%fused_computation.24 | loop fusion | flops 7340032 | bytes 16777216 | tf_op jit(solution)/shard_map/sub | solution.py:131
  108.1 2.0 %fusion = f32[256,64,64]{0,2,1:T(8,128)S(1)} fusion(f32[256,64,32]{0,2,1:T(8,128)S(1)} %get-tuple-element.4, f32[256,64,32]{0,2,1:T(8,128)S(1)} %get-tuple-element.3, f32[32,32]{0,1:T(8,128)S(1)} %get-tuple-element.26, f32[32,32]{0,1:T(8,128)S(1)} %fusion.66, f32[32,32]{0,1:T(8,128)S(1)} %get-tuple-element.25), kind=kOutput, calls=%fused_computation.3 | convolution fusion | flops 403714048 | bytes 8400896 | tf_op jit(solution)/shard_map/ckj,jn->ckn/dot_general | solution.py:72
  110.7 2.5 %multiply_subtract_fusion = (f32[256,64,32]{0,1,2:T(8,128)S(1)}, f32[256,64,32]{0,1,2:T(8,128)S(1)}) fusion(f32[256,64,32]{0,2,1:T(8,128)S(1)} %get-tuple-element.14, f32[256,64,32]{0,2,1:T(8,128)S(1)} %get-tuple-element.13, f32[64,32]{0,1:T(8,128)S(1)} %get-tuple-element.23, f32[64,32]{0,1:T(8,128)S(1)} %get-tuple-element.24), kind=kLoop, calls=%fused_computation.22 | loop fusion | flops 3145728 | bytes 8404992 | tf_op jit(solution)/shard_map/sub | solution.py:76
  113.2 1.6 multiply_bitcast_fusion
  117.8 1.6 copy.164
  122.2 18.1 %all_to_all.69 = bf16[8,2,16384]{2,1,0:T(2,128)(2,1)S(1)} all-to-all(bf16[8,2,16384]{2,1,0:T(2,128)(2,1)S(1)} %reshape.90), channel_id=1, replica_groups=mesh['seq'=8,'dp'=4] {'seq'}, dimensions={0} | all-to-all | bytes 1048576 | tf_op jit(solution)/shard_map/all_to_all | solution.py:133
  142.0 1.4 reduce-scatter.2.cloned.1.call-done
  145.3 2.0 %reduce = f32[1024,64]{1,0:T(8,128)S(1)} reduce(f32[1024,1,64]{2,1,0:T(1,128)S(1)} %bitcast.74, f32[]{:T(128)} %broadcast.101), dimensions={1}, to_apply=%bitcast.61.reduce_sub_computation | reduce | bytes 524292
  148.3 5.5 %all-to-all-start.4 = ((f32[8,1,8192]{2,1,0:T(1,128)}), f32[8,1,8192]{2,1,0:T(1,128)S(1)}, u32[]{:S(2)}, u32[]{:S(2)}) async-start(f32[8,1,8192]{2,1,0:T(1,128)} %reshape.92), calls=%async_computation.5 | async-start | bytes 524288 | tf_op jit(solution)/shard_map/all_to_all | solution.py:137
  155.0 7.6 %all-to-all-done.4 = f32[8,1,8192]{2,1,0:T(1,128)S(1)} async-done(((f32[8,1,8192]{2,1,0:T(1,128)}), f32[8,1,8192]{2,1,0:T(1,128)S(1)}, u32[]{:S(2)}, u32[]{:S(2)}) %all-to-all-start.4) | async-done | bytes 262176 | tf_op jit(solution)/shard_map/all_to_all | solution.py:137
  (58 shorter events, 27.1 us)
Async XLA Ops:
  7.2 9.9 %copy-start.6 = (bf16[1,2048,128]{2,1,0:T(8,128)(2,1)S(1)}, bf16[1,2048,128]{2,1,0:T(8,128)(2,1)}, u32[]{:S(2)}) copy-start(bf16[1,2048,128]{2,1,0:T(8,128)(2,1)} %param.6) | copy-start | bytes 1572868
  8.6 26.6 %copy-start.5 = (f32[2048,128]{1,0:T(8,128)S(1)}, f32[2048,128]{1,0:T(8,128)}, u32[]{:S(2)}) copy-start(f32[2048,128]{1,0:T(8,128)} %param.7) | copy-start | bytes 3145732
  9.8 21.8 %all-to-all-start.2 = ((bf16[4,512,128]{2,0,1:T(4,128)(2,1)}), bf16[4,512,128]{2,0,1:T(4,128)(2,1)S(1)}, u32[]{:S(2)}, u32[]{:S(2)}) async-start(bf16[4,512,128]{2,0,1:T(4,128)(2,1)} %copy.152), calls=%async_computation.2 | async-start | bytes 1048576 | tf_op jit(solution)/shard_map/all_to_all | solution.py:108
  31.6 18.3 %all-to-all-start.1 = ((bf16[4,512,128]{2,0,1:T(4,128)(2,1)}), bf16[4,512,128]{2,0,1:T(4,128)(2,1)S(1)}, u32[]{:S(2)}, u32[]{:S(2)}) async-start(bf16[4,512,128]{2,0,1:T(4,128)(2,1)} %copy.147), calls=%async_computation.1 | async-start | bytes 1048576 | tf_op jit(solution)/shard_map/all_to_all | solution.py:101
  49.9 4.5 %copy-start.4 = (bf16[4,512,128]{2,0,1:T(4,128)(2,1)}, bf16[4,512,128]{2,0,1:T(4,128)(2,1)S(1)}, u32[]{:S(2)}) copy-start(bf16[4,512,128]{2,0,1:T(4,128)(2,1)S(1)} %all-to-all-done.1) | copy-start | bytes 1572868
  49.9 29.6 %all-to-all-start = ((f32[4,512,128]{2,0,1:T(4,128)}), f32[4,512,128]{2,0,1:T(4,128)S(1)}, u32[]{:S(2)}, u32[]{:S(2)}) async-start(f32[4,512,128]{2,0,1:T(4,128)} %copy.142), calls=%async_computation | async-start | bytes 2097152 | tf_op jit(solution)/shard_map/all_to_all | solution.py:117
  53.5 89.9 %reduce-scatter.2.cloned.1.call-start = ((), (), s32[]{:S(2)}) async-start(), calls=%async_computation.6 | async-start | bytes 1310720 | tf_op jit(solution)/shard_map/reduce_scatter | solution.py:136
  81.6 3.7 %copy-start = (f32[256,128,32]{0,1,2:T(8,128)S(1)}, f32[256,128,32]{0,1,2:T(8,128)}, u32[]{:S(2)}) copy-start(f32[256,128,32]{0,1,2:T(8,128)} %convolution_bitcast_fusion) | copy-start | bytes 12582916
  114.8 1.3 copy-start.1
  142.0 11.8 %copy-start.2 = (bf16[1,2048,128]{2,1,0:T(8,128)(2,1)S(1)}, bf16[1,2048,128]{2,1,0:T(8,128)(2,1)}, u32[]{:S(2)}) copy-start(bf16[1,2048,128]{2,1,0:T(8,128)(2,1)} %param.5) | copy-start | bytes 1572868
  142.0 11.8 %copy-start.3 = (bf16[1,2048,128]{2,1,0:T(8,128)(2,1)S(1)}, bf16[1,2048,128]{2,1,0:T(8,128)(2,1)}, u32[]{:S(2)}) copy-start(bf16[1,2048,128]{2,1,0:T(8,128)(2,1)} %param.4) | copy-start | bytes 1572868
  148.3 14.3 %all-to-all-start.4 = ((f32[8,1,8192]{2,1,0:T(1,128)}), f32[8,1,8192]{2,1,0:T(1,128)S(1)}, u32[]{:S(2)}, u32[]{:S(2)}) async-start(f32[8,1,8192]{2,1,0:T(1,128)} %reshape.92), calls=%async_computation.5 | async-start | bytes 524288 | tf_op jit(solution)/shard_map/all_to_all | solution.py:137
Sparse Core Ops, SparseCore 0:
  119.6 23.8 reduce-scatter.1
where the time goes:
time: 176 us; the launch traced here: 173 us
  waiting for transfers between devices  49.8 us (28%)
  matrix products  29.6 us (17%)
  local copies, waits for them, and re-layouts  24.3 us (14%)
  starting transfers between devices  20.3 us (12%)
  blocking collectives  18.1 us (10%)
  other arithmetic  16 us (9%)
  between operations  14.6 us (8%)
    all_to_all x1, blocking collectives, shards(): lax.all_to_all(carried, 'seq', split_axis=2, concat_axis=1, tiled=True)  18.1 us
    dot_general x3, matrix products, spectrum(): out = jnp.einsum('ckn,nj->ckj', turned, last_fwd, precision=first_precision)  15.6 us
    all_to_all x1, waiting for transfers between devices, shards(): lax.all_to_all(filter_grouped, 'seq', split_axis=1, concat_axis=2, tiled=...  14.6 us
    all_to_all x1, waiting for transfers between devices, shards(): lax.all_to_all(mixed.reshape(group_count, quarter, shard_len), 'seq', spl...  13.3 us
    all_to_all x1, waiting for transfers between devices, shards(): lax.all_to_all(out_grad[0].reshape(group_count, quarter, shard_len), 'seq...  12.9 us
    dot_general x3, matrix products, spectrum(): part = jnp.einsum('cmn,mk->ckn', grid, first_fwd, precision=first_precision)  10.4 us
    all_to_all x1, waiting for transfers between devices, shards(): lax.all_to_all(summed, 'seq', split_axis=2, concat_axis=1, tiled=True)  7.55 us
    all_to_all x1, starting transfers between devices, shards(): lax.all_to_all(mixed.reshape(group_count, quarter, shard_len), 'seq', spl...  7.31 us
  transfers between devices with their start and end apart: 5, of which 5 were waited for; matrix products, arithmetic and copies ran while one was open for 11% of the time, Pallas kernels for 0%

commit v1 on v0

--- a/solution.py
+++ b/solution.py
@@ -1,9 +1,16 @@
+import functools
 import math
 
 import jax
 import jax.numpy as jnp
 from jax import lax
+from jax.experimental import pallas as pl
+from jax.experimental.pallas import tpu as pltpu
 from jax.sharding import PartitionSpec as P
+
+LANES = 128
+SUBLANES = 16
+ROOM = 40 * 2**20
 
 precise = lax.Precision.HIGHEST
 coarse = lax.Precision.HIGH
@@ -83,7 +90,7 @@
     return (real_part.reshape(held, length), imag_part.reshape(held, length))
 
 
-def shards(gate_in, values_in, out_grad, filter_taps):
+def spectral_shards(gate_in, values_in, out_grad, filter_taps):
     seq_count = lax.axis_size("seq")
     group_count = lax.axis_size("dp")
     channels = gate_in.shape[1]
@@ -142,6 +149,177 @@
     return (grad_gate, grad_values, grad_filter)
 
 
+def pack_body(groups, peers, own_ref, gate_ref, values_ref, grad_ref, taps_ref, out_ref):
+    part = out_ref.shape[1] // (2 * groups + 2)
+    half = groups * part
+    for q in range(groups):
+        rows = pl.ds(q * peers * part, peers * part)
+        mixed = gate_ref[rows, :].astype(jnp.float32) * values_ref[rows, :].astype(jnp.float32)
+        out_ref[:, q * part : (q + 1) * part, :] = grad_ref[rows, :].reshape(peers, part, LANES)
+        out_ref[:, half + q * part : half + (q + 1) * part, :] = mixed.astype(jnp.bfloat16).reshape(
+            peers, part, LANES
+        )
+    first = pl.multiple_of(own_ref[0] * (peers * part), peers * part)
+    taps = taps_ref[pl.ds(first, peers * part), :]
+    high = taps.astype(jnp.bfloat16)
+    low = (taps - high.astype(jnp.float32)).astype(jnp.bfloat16)
+    out_ref[:, 2 * half : 2 * half + part, :] = high.reshape(peers, part, LANES)
+    out_ref[:, 2 * half + part :, :] = low.reshape(peers, part, LANES)
+
+
+def correlate_body(seqs, blocks, in_ref, out_ref, gs, ms, fs, cs, rs):
+    peers = seqs * blocks
+    part = in_ref.shape[1] // (2 * seqs + 2)
+    held = seqs * part
+    row = lax.broadcasted_iota(jnp.int32, (LANES, LANES), 0)
+    lane = lax.broadcasted_iota(jnp.int32, (LANES, LANES), 1)
+    flip = jnp.where(row + lane == LANES - 1, 1.0, 0.0).astype(jnp.bfloat16)
+    same = lane <= row
+    ahead = lane >= row
+    span = blocks * held
+    for b in range(seqs):
+        mine = slice(b * blocks, (b + 1) * blocks)
+        gs[pl.ds(2 * b * span, span), :] = (
+            in_ref[mine, :held, :].astype(jnp.float32).reshape(span, LANES)
+        )
+        gs[pl.ds((2 * b + 1) * span, span), :] = jnp.zeros((span, LANES), jnp.float32)
+        ms[pl.ds(b * span, span), :] = (
+            in_ref[mine, held : 2 * held, :].astype(jnp.float32).reshape(span, LANES)
+        )
+        for s in range(blocks):
+            high = in_ref[b * blocks + s, 2 * held : 2 * held + part, :].astype(jnp.float32)
+            low = in_ref[b * blocks + s, 2 * held + part :, :].astype(jnp.float32)
+            fs[pl.ds(s * held + b * part, part), :] = high + low
+
+    def channel(c, carry):
+        shifted = []
+        for k in range(blocks):
+            parts = [
+                gs[pl.ds((2 * b * blocks + k) * held + c, blocks, stride=held), :] for b in range(seqs)
+            ]
+            shifted.append(jnp.concatenate(parts, axis=0).astype(jnp.bfloat16))
+        hankel = jnp.concatenate(shifted, axis=1)
+        mixed = ms[pl.ds(c, peers, stride=held), :].astype(jnp.bfloat16)
+        dims = (((1,), (1,)), ((), ()))
+        turned = lax.dot_general(flip, mixed, dims, preferred_element_type=jnp.float32).astype(
+            jnp.bfloat16
+        )
+        gram = jnp.dot(turned, hankel, preferred_element_type=jnp.float32)
+        rolled = [
+            pltpu.roll(gram[:, k * LANES : (k + 1) * LANES], 1, 1, stride=1, stride_axis=0)
+            for k in range(blocks)
+        ]
+        rolled.append(jnp.zeros((LANES, LANES), jnp.float32))
+        sums = [
+            jnp.sum(jnp.where(same, rolled[k], rolled[k + 1]), axis=0, keepdims=True)
+            for k in range(blocks)
+        ]
+        rs[pl.ds(c, blocks, stride=held), :] = jnp.concatenate(sums, axis=0)
+        taps = fs[pl.ds(c, blocks, stride=held), :]
+        before = jnp.zeros((LANES, LANES), jnp.float32)
+        high, low = [], []
+        for k in range(blocks):
+            turn = pltpu.roll(
+                jnp.broadcast_to(taps[k : k + 1, :], (LANES, LANES)), 0, 1, stride=1, stride_axis=0
+            )
+            block = jnp.where(ahead, turn, before)
+            before = turn
+            top = block.astype(jnp.bfloat16)
+            high.append(top)
+            low.append((block - top.astype(jnp.float32)).astype(jnp.bfloat16))
+        carried = lax.dot_general(
+            hankel, jnp.concatenate(high, axis=1), dims, preferred_element_type=jnp.float32
+        ) + lax.dot_general(
+            hankel, jnp.concatenate(low, axis=1), dims, preferred_element_type=jnp.float32
+        )
+        cs[pl.ds(c, peers, stride=held), :] = carried
+        return carry
+
+    lax.fori_loop(0, held, channel, 0)
+    out_ref[:, :held, :] = cs[...].reshape(peers, held, LANES).astype(jnp.bfloat16)
+    for q in range(seqs):
+        for s in range(blocks):
+            out_ref[q * blocks + s, held:, :] = rs[pl.ds(s * held + q * part, part), :].astype(
+                jnp.bfloat16
+            )
+
+
+def unpack_body(groups, in_ref, gate_ref, values_ref, gate_out, values_out, filter_out):
+    peers = in_ref.shape[0]
+    part = in_ref.shape[1] // (groups + 1)
+    for q in range(groups):
+        rows = pl.ds(q * peers * part, peers * part)
+        carried = (
+            in_ref[:, q * part : (q + 1) * part, :].astype(jnp.float32).reshape(peers * part, LANES)
+        )
+        gate_out[rows, :] = (carried * values_ref[rows, :].astype(jnp.float32)).astype(jnp.bfloat16)
+        values_out[rows, :] = (carried * gate_ref[rows, :].astype(jnp.float32)).astype(jnp.bfloat16)
+    filter_out[...] = (
+        in_ref[:, groups * part :, :].astype(jnp.float32).reshape(peers * part, LANES)
+    )
+
+
+def correlate(arrived, seqs):
+    peers, rows, _ = arrived.shape
+    blocks = peers // seqs
+    part = rows // (2 * seqs + 2)
+    held = seqs * part
+    whole = pl.BlockSpec(memory_space=pltpu.VMEM)
+    return pl.pallas_call(
+        functools.partial(correlate_body, seqs, blocks),
+        out_shape=jax.ShapeDtypeStruct((peers, held + part, LANES), jnp.bfloat16),
+        in_specs=[whole],
+        out_specs=whole,
+        scratch_shapes=[
+            pltpu.VMEM((2 * peers * held, LANES), jnp.float32),
+            pltpu.VMEM((peers * held, LANES), jnp.float32),
+            pltpu.VMEM((blocks * held, LANES), jnp.float32),
+            pltpu.VMEM((peers * held, LANES), jnp.float32),
+            pltpu.VMEM((blocks * held, LANES), jnp.float32),
+        ],
+        cost_estimate=pl.CostEstimate(
+            flops=6 * held * LANES * blocks * LANES * peers, bytes_accessed=4 * arrived.size, transcendentals=0
+        ),
+    )(arrived)
+
+
+def direct_shards(gate_in, values_in, out_grad, filter_taps):
+    groups = lax.axis_size("dp")
+    peers = groups * lax.axis_size("seq")
+    channels = gate_in.shape[1]
+    part = channels // (groups * peers)
+    whole = pl.BlockSpec(memory_space=pltpu.VMEM)
+    own = lax.axis_index("dp").astype(jnp.int32).reshape(1)
+    packed = pl.pallas_call(
+        functools.partial(pack_body, groups, peers),
+        out_shape=jax.ShapeDtypeStruct((peers, (2 * groups + 2) * part, LANES), jnp.bfloat16),
+        in_specs=[pl.BlockSpec(memory_space=pltpu.SMEM), whole, whole, whole, whole],
+        out_specs=whole,
+    )(own, gate_in[0], values_in[0], out_grad[0], filter_taps)
+    arrived = lax.all_to_all(packed, ("dp", "seq"), split_axis=0, concat_axis=0, tiled=True)
+    made = correlate(arrived, groups)
+    home = lax.all_to_all(made, ("dp", "seq"), split_axis=0, concat_axis=0, tiled=True)
+    wide = jax.ShapeDtypeStruct((channels, LANES), jnp.bfloat16)
+    grad_gate, grad_values, grad_filter = pl.pallas_call(
+        functools.partial(unpack_body, groups),
+        out_shape=(wide, wide, jax.ShapeDtypeStruct((channels // groups, LANES), jnp.float32)),
+        in_specs=[whole, whole, whole],
+        out_specs=(whole, whole, whole),
+    )(home, gate_in[0], values_in[0])
+    return (grad_gate[None], grad_values[None], grad_filter)
+
+
+def shards(gate_in, values_in, out_grad, filter_taps):
+    groups = lax.axis_size("dp")
+    peers = groups * lax.axis_size("seq")
+    channels, shard_len = gate_in.shape[1:]
+    part = channels // (groups * peers)
+    fits = 24 * channels * LANES * groups <= ROOM
+    if shard_len == LANES and channels == part * groups * peers and part % SUBLANES == 0 and fits:
+        return direct_shards(gate_in, values_in, out_grad, filter_taps)
+    return spectral_shards(gate_in, values_in, out_grad, filter_taps)
+
+
 def solution(mesh):
     return jax.shard_map(
         shards,

time: 176 us -> 107 us (0.61); the launches traced: 173 us -> 106 us
  waiting for transfers between devices: 49.8 us -> 0 us
  blocking collectives: 18.1 us -> 62.9 us
  Pallas kernels: 0 us -> 42.7 us
  matrix products: 29.6 us -> 0 us
  local copies, waits for them, and re-layouts: 24.3 us -> 0 us
  starting transfers between devices: 20.3 us -> 0 us
  other arithmetic: 16 us -> 0 us
  between operations: 14.6 us -> 0.64 us
    all_to_all x4 -> x0, waiting for transfers between devices: 48.3 us -> none  [the longest x1 14.6 us: shards(): lax.all_to_all(filter_grouped, 'seq', split_axis=1, concat_axis=2, tiled=...]
    all_to_all x1 -> x2, blocking collectives: 18.1 us -> 62.9 us  [the longest x1 40.5 us: direct_shards(): lax.all_to_all(packed, ('dp', 'seq'), split_axis=0, concat_axis=0, tiled=...]
    pallas_call x0 -> x3, Pallas kernels: none -> 42.7 us  [the longest x1 37.2 us: correlate(): pl.pallas_call(functools.partial(correlate_body, seqs, blocks), out_shape...]
    dot_general x8 -> x0, matrix products: 29.6 us -> none  [the longest x3 15.6 us: spectrum(): out = jnp.einsum('ckn,nj->ckj', turned, last_fwd, precision=first_precision)]
    all_to_all x4 -> x0, starting transfers between devices: 20.1 us -> none  [the longest x1 7.31 us: shards(): lax.all_to_all(mixed.reshape(group_count, quarter, shard_len), 'seq', spl...]
    all_to_all x9 -> x0, local copies, waits for them, and re-layouts: 5.3 us -> none  [the longest x2 1.81 us: shards(): lax.all_to_all(out_grad[0].reshape(group_count, quarter, shard_len), 'seq...]
    unnamed x20 -> x0, local copies, waits for them, and re-layouts: 5.07 us -> none
    another operation x4 -> x0, local copies, waits for them, and re-layouts: 5.02 us -> none  [the longest x2 2.69 us: shards(): lagged = lagged.reshape(group_count, per_block, length)]
  transfers between devices with their start and end apart: 5 -> 0, of which waited for: 5 -> 0; matrix products, arithmetic and copies ran while one was open for 11% -> 0% of each run, Pallas kernels for 0% -> 0%
where the time goes in v1:
time: 107 us; the launch traced here: 106 us
  blocking collectives  62.9 us (59%)
  Pallas kernels  42.7 us (40%)
    all_to_all x1, blocking collectives, direct_shards(): lax.all_to_all(packed, ('dp', 'seq'), split_axis=0, concat_axis=0, tiled=...  40.5 us
    pallas_call x1, Pallas kernels, correlate(): pl.pallas_call(functools.partial(correlate_body, seqs, blocks), out_shape...  37.2 us
    all_to_all x1, blocking collectives, direct_shards(): lax.all_to_all(made, ('dp', 'seq'), split_axis=0, concat_axis=0, tiled=True)  22.4 us
    pallas_call x1, Pallas kernels, direct_shards(): pl.pallas_call(functools.partial(pack_body, groups, peers), out_shape=jax...  2.97 us
    pallas_call x1, Pallas kernels, direct_shards(): pl.pallas_call(functools.partial(unpack_body, groups), out_shape=(wide, w...  2.57 us

profile of v1, /device:TPU:0, one launch (start us, length us, event | category | flops | bytes accessed | tf_op | source)
XLA Modules:
  0.0 106.2 jit_solution(13379006820060102838)
XLA Ops:
  0.6 3.0 %shard_map.67 = bf16[32,160,128]{2,1,0:T(8,128)(2,1)} custom-call(s32[1]{0:T(128)} %bitcast.own_ref, bf16[2048,128]{1,0:T(8,128)(2,1)} %bitcast.6, bf16[2048,128]{1,0:T(8,128)(2,1)} %bitcast.8, bf16[2048,128]{1,0:T(8,128)(2,1)} %bitcast.10, f32[2048,128]{1,0:T(8,128)} %taps_ref.1), custom_call_target="tpu_custom_call" | custom-call | tf_op jit(solution)/shard_map/pallas_call | solution.py:293
  3.6 40.5 %all_to_all.10.in_ref = bf16[32,160,128]{2,1,0:T(8,128)(2,1)} all-to-all(bf16[32,160,128]{2,1,0:T(8,128)(2,1)} %shard_map.67), channel_id=1, replica_groups=mesh['seq'=8,'dp'=4] {'dp','seq'}, dimensions={0} | all-to-all | bytes 2621440 | tf_op jit(solution)/shard_map/all_to_all | solution.py:299
  44.1 37.2 %shard_map.68 = bf16[32,80,128]{2,1,0:T(8,128)(2,1)} custom-call(bf16[32,160,128]{2,1,0:T(8,128)(2,1)} %all_to_all.10.in_ref), custom_call_target="tpu_custom_call" | custom-call | flops 1610612736 | bytes 2621440 | tf_op jit(solution)/shard_map/pallas_call | solution.py:268
  81.3 22.4 %all_to_all.11.in_ref = bf16[32,80,128]{2,1,0:T(8,128)(2,1)} all-to-all(bf16[32,80,128]{2,1,0:T(8,128)(2,1)} %shard_map.68), channel_id=1, replica_groups=mesh['seq'=8,'dp'=4] {'dp','seq'}, dimensions={0} | all-to-all | bytes 1310720 | tf_op jit(solution)/shard_map/all_to_all | solution.py:301
  103.7 2.6 %shard_map.69 = (bf16[2048,128]{1,0:T(8,128)(2,1)}, bf16[2048,128]{1,0:T(8,128)(2,1)}, f32[512,128]{1,0:T(8,128)}) custom-call(bf16[32,80,128]{2,1,0:T(8,128)(2,1)} %all_to_all.11.in_ref, bf16[2048,128]{1,0:T(8,128)(2,1)} %bitcast.7, bf16[2048,128]{1,0:T(8,128)(2,1)} %bitcast.9), custom_call_target="tpu_custom_call" | custom-call | tf_op jit(solution)/shard_map/pallas_call | solution.py:303

commit v2 on v1

--- a/solution.py
+++ b/solution.py
@@ -10,6 +10,8 @@
 
 LANES = 128
 SUBLANES = 16
+REACH = 32
+UNROLL = 8
 ROOM = 40 * 2**20
 
 precise = lax.Precision.HIGHEST
@@ -167,22 +169,25 @@
     out_ref[:, 2 * half + part :, :] = low.reshape(peers, part, LANES)
 
 
-def correlate_body(seqs, blocks, in_ref, out_ref, gs, ms, fs, cs, rs):
+def correlate_body(seqs, blocks, unroll, in_ref, out_ref, gs, ms, fs, cs, rs, pads, hs, ts):
     peers = seqs * blocks
     part = in_ref.shape[1] // (2 * seqs + 2)
     held = seqs * part
-    row = lax.broadcasted_iota(jnp.int32, (LANES, LANES), 0)
-    lane = lax.broadcasted_iota(jnp.int32, (LANES, LANES), 1)
-    flip = jnp.where(row + lane == LANES - 1, 1.0, 0.0).astype(jnp.bfloat16)
-    same = lane <= row
-    ahead = lane >= row
+    steps = LANES // REACH
+    near = lax.broadcasted_iota(jnp.int32, (REACH, LANES), 0)
+    lane = lax.broadcasted_iota(jnp.int32, (REACH, LANES), 1)
+    flip = jnp.where(lane % REACH + near == REACH - 1, 1.0, 0.0).astype(jnp.bfloat16)
+    ours = lax.broadcasted_iota(jnp.int32, (peers, LANES), 1) // REACH
+    inside = lane + REACH - 1 - near < LANES
+    ahead = lane >= near
+    thin = lax.broadcasted_iota(jnp.int32, (blocks, LANES), 1)
+    across = (((1,), (1,)), ((), ()))
     span = blocks * held
     for b in range(seqs):
         mine = slice(b * blocks, (b + 1) * blocks)
-        gs[pl.ds(2 * b * span, span), :] = (
+        gs[pl.ds(b * span, span), :] = (
             in_ref[mine, :held, :].astype(jnp.float32).reshape(span, LANES)
         )
-        gs[pl.ds((2 * b + 1) * span, span), :] = jnp.zeros((span, LANES), jnp.float32)
         ms[pl.ds(b * span, span), :] = (
             in_ref[mine, held : 2 * held, :].astype(jnp.float32).reshape(span, LANES)
         )
@@ -190,52 +195,90 @@
             high = in_ref[b * blocks + s, 2 * held : 2 * held + part, :].astype(jnp.float32)
             low = in_ref[b * blocks + s, 2 * held + part :, :].astype(jnp.float32)
             fs[pl.ds(s * held + b * part, part), :] = high + low
-
-    def channel(c, carry):
-        shifted = []
-        for k in range(blocks):
-            parts = [
-                gs[pl.ds((2 * b * blocks + k) * held + c, blocks, stride=held), :] for b in range(seqs)
-            ]
-            shifted.append(jnp.concatenate(parts, axis=0).astype(jnp.bfloat16))
-        hankel = jnp.concatenate(shifted, axis=1)
-        mixed = ms[pl.ds(c, peers, stride=held), :].astype(jnp.bfloat16)
-        dims = (((1,), (1,)), ((), ()))
-        turned = lax.dot_general(flip, mixed, dims, preferred_element_type=jnp.float32).astype(
-            jnp.bfloat16
-        )
-        gram = jnp.dot(turned, hankel, preferred_element_type=jnp.float32)
-        rolled = [
-            pltpu.roll(gram[:, k * LANES : (k + 1) * LANES], 1, 1, stride=1, stride_axis=0)
-            for k in range(blocks)
-        ]
-        rolled.append(jnp.zeros((LANES, LANES), jnp.float32))
-        sums = [
-            jnp.sum(jnp.where(same, rolled[k], rolled[k + 1]), axis=0, keepdims=True)
-            for k in range(blocks)
-        ]
-        rs[pl.ds(c, blocks, stride=held), :] = jnp.concatenate(sums, axis=0)
-        taps = fs[pl.ds(c, blocks, stride=held), :]
-        before = jnp.zeros((LANES, LANES), jnp.float32)
-        high, low = [], []
-        for k in range(blocks):
-            turn = pltpu.roll(
-                jnp.broadcast_to(taps[k : k + 1, :], (LANES, LANES)), 0, 1, stride=1, stride_axis=0
+    pads[...] = jnp.zeros_like(pads)
+
+    def at(u, q, b):
+        return ((u * steps + q) * seqs + b) * 2 * blocks
+
+    def several(i, carry):
+        lot = [(u, i * unroll + u) for u in range(unroll)]
+        for u, c in lot:
+            for b in range(seqs):
+                pads[pl.ds(at(u, 0, b), blocks), :] = gs[pl.ds(b * span + c, blocks, stride=held), :]
+        turned = []
+        for u, c in lot:
+            mixed = ms[pl.ds(c, peers, stride=held), :]
+            mixed = jnp.concatenate(
+                [jnp.where(ours == q, mixed, 0.0).astype(jnp.bfloat16) for q in range(steps)], axis=0
             )
-            block = jnp.where(ahead, turn, before)
-            before = turn
-            top = block.astype(jnp.bfloat16)
-            high.append(top)
-            low.append((block - top.astype(jnp.float32)).astype(jnp.bfloat16))
-        carried = lax.dot_general(
-            hankel, jnp.concatenate(high, axis=1), dims, preferred_element_type=jnp.float32
-        ) + lax.dot_general(
-            hankel, jnp.concatenate(low, axis=1), dims, preferred_element_type=jnp.float32
-        )
-        cs[pl.ds(c, peers, stride=held), :] = carried
+            turned.append(
+                lax.dot_general(flip, mixed, across, preferred_element_type=jnp.float32).astype(
+                    jnp.bfloat16
+                )
+            )
+        for u, c in lot:
+            for q in range(1, steps):
+                for b in range(seqs):
+                    here = pads[pl.ds(at(u, 0, b), blocks), :]
+                    then = pads[pl.ds(at(u, 0, b) + 1, blocks), :]
+                    pads[pl.ds(at(u, q, b), blocks), :] = pltpu.roll(
+                        jnp.where(thin >= q * REACH, here, then), LANES - q * REACH, 1
+                    )
+        for u, c in lot:
+            taps = fs[pl.ds(c, blocks, stride=held), :]
+            before = jnp.zeros((REACH, LANES), jnp.float32)
+            for k in range(blocks):
+                turn = pltpu.roll(
+                    jnp.broadcast_to(taps[k : k + 1, :], (REACH, LANES)),
+                    0,
+                    1,
+                    stride=1,
+                    stride_axis=0,
+                )
+                block = jnp.where(ahead, turn, before)
+                before = turn
+                top = block.astype(jnp.bfloat16)
+                ts[u, :REACH, k * LANES : (k + 1) * LANES] = top
+                ts[u, REACH:, k * LANES : (k + 1) * LANES] = (
+                    block - top.astype(jnp.float32)
+                ).astype(jnp.bfloat16)
+        for u, c in lot:
+            for q in range(steps):
+                for k in range(blocks):
+                    hs[u, q * peers : (q + 1) * peers, k * LANES : (k + 1) * LANES] = jnp.concatenate(
+                        [pads[pl.ds(at(u, q, b) + k, blocks), :] for b in range(seqs)], axis=0
+                    ).astype(jnp.bfloat16)
+        for u, c in lot:
+            gram = jnp.dot(turned[u], hs[u], preferred_element_type=jnp.float32)
+            later = jnp.zeros((REACH, LANES), jnp.float32)
+            sums = []
+            for k in reversed(range(blocks)):
+                turn = pltpu.roll(
+                    gram[:, k * LANES : (k + 1) * LANES],
+                    LANES + 1 - REACH,
+                    1,
+                    stride=1,
+                    stride_axis=0,
+                )
+                sums.append(jnp.sum(jnp.where(inside, turn, later), axis=0, keepdims=True))
+                later = turn
+            rs[pl.ds(c, blocks, stride=held), :] = jnp.concatenate(sums[::-1], axis=0)
+        for u, c in lot:
+            short = lax.dot_general(hs[u], ts[u], across, preferred_element_type=jnp.float32)
+            short = jnp.concatenate(
+                [short, jnp.zeros((steps * peers, LANES - 2 * REACH), jnp.float32)], axis=1
+            )
+            carried = None
+            for q in range(steps):
+                mine = short[q * peers : (q + 1) * peers]
+                both = pltpu.roll(mine, q * REACH, 1) if q else mine
+                back = (q - 1) % steps
+                both = both + (pltpu.roll(mine, back * REACH, 1) if back else mine)
+                carried = both if carried is None else jnp.where(ours == q, both, carried)
+            cs[pl.ds(c, peers, stride=held), :] = carried
         return carry
 
-    lax.fori_loop(0, held, channel, 0)
+    lax.fori_loop(0, held // unroll, several, 0)
     out_ref[:, :held, :] = cs[...].reshape(peers, held, LANES).astype(jnp.bfloat16)
     for q in range(seqs):
         for s in range(blocks):
@@ -266,16 +309,19 @@
     held = seqs * part
     whole = pl.BlockSpec(memory_space=pltpu.VMEM)
     return pl.pallas_call(
-        functools.partial(correlate_body, seqs, blocks),
+        functools.partial(correlate_body, seqs, blocks, UNROLL),
         out_shape=jax.ShapeDtypeStruct((peers, held + part, LANES), jnp.bfloat16),
         in_specs=[whole],
         out_specs=whole,
         scratch_shapes=[
-            pltpu.VMEM((2 * peers * held, LANES), jnp.float32),
+            pltpu.VMEM((peers * held, LANES), jnp.float32),
             pltpu.VMEM((peers * held, LANES), jnp.float32),
             pltpu.VMEM((blocks * held, LANES), jnp.float32),
             pltpu.VMEM((peers * held, LANES), jnp.float32),
             pltpu.VMEM((blocks * held, LANES), jnp.float32),
+            pltpu.VMEM((UNROLL * (LANES // REACH) * 2 * peers, LANES), jnp.float32),
+            pltpu.VMEM((UNROLL, LANES // REACH * peers, blocks * LANES), jnp.bfloat16),
+            pltpu.VMEM((UNROLL, 2 * REACH, blocks * LANES), jnp.bfloat16),
         ],
         cost_estimate=pl.CostEstimate(
             flops=6 * held * LANES * blocks * LANES * peers, bytes_accessed=4 * arrived.size, transcendentals=0

time: 107 us -> 86.1 us (0.80)
  Pallas kernels: 42.7 us -> 22.2 us
    pallas_call x1, Pallas kernels: 37.2 us -> 16.6 us  [correlate(): pl.pallas_call(functools.partial(correlate_body, seqs, blocks, UNROLL), o...]
where the time goes in v2:
time: 86.1 us; the launch traced here: 85.7 us
  blocking collectives  62.9 us (73%)
  Pallas kernels  22.2 us (26%)
    all_to_all x1, blocking collectives, direct_shards(): lax.all_to_all(packed, ('dp', 'seq'), split_axis=0, concat_axis=0, tiled=...  40.5 us
    all_to_all x1, blocking collectives, direct_shards(): lax.all_to_all(made, ('dp', 'seq'), split_axis=0, concat_axis=0, tiled=True)  22.4 us
    pallas_call x1, Pallas kernels, correlate(): pl.pallas_call(functools.partial(correlate_body, seqs, blocks, UNROLL), o...  16.6 us
    pallas_call x1, Pallas kernels, direct_shards(): pl.pallas_call(functools.partial(pack_body, groups, peers), out_shape=jax...  2.97 us
    pallas_call x1, Pallas kernels, direct_shards(): pl.pallas_call(functools.partial(unpack_body, groups), out_shape=(wide, w...  2.57 us

profile of v2, /device:TPU:0, one launch (start us, length us, event | category | flops | bytes accessed | tf_op | source)
XLA Modules:
  0.0 85.7 jit_solution(2468611645368000235)
XLA Ops:
  0.6 3.0 %shard_map.67 = bf16[32,160,128]{2,1,0:T(8,128)(2,1)} custom-call(s32[1]{0:T(128)} %bitcast.own_ref, bf16[2048,128]{1,0:T(8,128)(2,1)} %bitcast.6, bf16[2048,128]{1,0:T(8,128)(2,1)} %bitcast.8, bf16[2048,128]{1,0:T(8,128)(2,1)} %bitcast.10, f32[2048,128]{1,0:T(8,128)} %taps_ref.1), custom_call_target="tpu_custom_call" | custom-call | tf_op jit(solution)/shard_map/pallas_call | solution.py:339
  3.6 40.5 %all_to_all.10.in_ref = bf16[32,160,128]{2,1,0:T(8,128)(2,1)} all-to-all(bf16[32,160,128]{2,1,0:T(8,128)(2,1)} %shard_map.67), channel_id=1, replica_groups=mesh['seq'=8,'dp'=4] {'dp','seq'}, dimensions={0} | all-to-all | bytes 2621440 | tf_op jit(solution)/shard_map/all_to_all | solution.py:345
  44.1 16.6 %shard_map.68 = bf16[32,80,128]{2,1,0:T(8,128)(2,1)} custom-call(bf16[32,160,128]{2,1,0:T(8,128)(2,1)} %all_to_all.10.in_ref), custom_call_target="tpu_custom_call" | custom-call | flops 1610612736 | bytes 2621440 | tf_op jit(solution)/shard_map/pallas_call | solution.py:311
  60.8 22.4 %all_to_all.11.in_ref = bf16[32,80,128]{2,1,0:T(8,128)(2,1)} all-to-all(bf16[32,80,128]{2,1,0:T(8,128)(2,1)} %shard_map.68), channel_id=1, replica_groups=mesh['seq'=8,'dp'=4] {'dp','seq'}, dimensions={0} | all-to-all | bytes 1310720 | tf_op jit(solution)/shard_map/all_to_all | solution.py:347
  83.1 2.6 %shard_map.69 = (bf16[2048,128]{1,0:T(8,128)(2,1)}, bf16[2048,128]{1,0:T(8,128)(2,1)}, f32[512,128]{1,0:T(8,128)}) custom-call(bf16[32,80,128]{2,1,0:T(8,128)(2,1)} %all_to_all.11.in_ref, bf16[2048,128]{1,0:T(8,128)(2,1)} %bitcast.7, bf16[2048,128]{1,0:T(8,128)(2,1)} %bitcast.9), custom_call_target="tpu_custom_call" | custom-call | tf_op jit(solution)/shard_map/pallas_call | solution.py:349

commit v3 on v2

--- a/solution.py
+++ b/solution.py
@@ -151,28 +151,38 @@
     return (grad_gate, grad_values, grad_filter)
 
 
-def pack_body(groups, peers, own_ref, gate_ref, values_ref, grad_ref, taps_ref, out_ref):
-    part = out_ref.shape[1] // (2 * groups + 2)
-    half = groups * part
-    for q in range(groups):
-        rows = pl.ds(q * peers * part, peers * part)
+def pack_body(groups, peers, first, count, own_ref, gate_ref, values_ref, grad_ref, taps_ref, out_ref):
+    part = gate_ref.shape[0] // (groups * peers)
+    half = count * part
+    for i in range(count):
+        rows = pl.ds((first + i) * peers * part, peers * part)
         mixed = gate_ref[rows, :].astype(jnp.float32) * values_ref[rows, :].astype(jnp.float32)
-        out_ref[:, q * part : (q + 1) * part, :] = grad_ref[rows, :].reshape(peers, part, LANES)
-        out_ref[:, half + q * part : half + (q + 1) * part, :] = mixed.astype(jnp.bfloat16).reshape(
+        out_ref[:, i * part : (i + 1) * part, :] = grad_ref[rows, :].reshape(peers, part, LANES)
+        out_ref[:, half + i * part : half + (i + 1) * part, :] = mixed.astype(jnp.bfloat16).reshape(
             peers, part, LANES
         )
-    first = pl.multiple_of(own_ref[0] * (peers * part), peers * part)
-    taps = taps_ref[pl.ds(first, peers * part), :]
-    high = taps.astype(jnp.bfloat16)
-    low = (taps - high.astype(jnp.float32)).astype(jnp.bfloat16)
-    out_ref[:, 2 * half : 2 * half + part, :] = high.reshape(peers, part, LANES)
-    out_ref[:, 2 * half + part :, :] = low.reshape(peers, part, LANES)
-
-
-def correlate_body(seqs, blocks, unroll, in_ref, out_ref, gs, ms, fs, cs, rs, pads, hs, ts):
+    if not first:
+        start = pl.multiple_of(own_ref[0] * (peers * part), peers * part)
+        taps = taps_ref[pl.ds(start, peers * part), :]
+        high = taps.astype(jnp.bfloat16)
+        low = (taps - high.astype(jnp.float32)).astype(jnp.bfloat16)
+        out_ref[:, 2 * half : 2 * half + part, :] = high.reshape(peers, part, LANES)
+        out_ref[:, 2 * half + part :, :] = low.reshape(peers, part, LANES)
+
+
+def correlate_body(
+    seqs, blocks, unroll, part, first, count, *refs
+):
     peers = seqs * blocks
-    part = in_ref.shape[1] // (2 * seqs + 2)
-    held = seqs * part
+    held = count * part
+    in_ref, taps_ref, *refs = refs
+    past_ref = None
+    if first:
+        past_ref, *refs = refs
+        out_ref, *refs = refs
+    else:
+        out_ref, sum_ref, *refs = refs
+    gs, ms, fs, cs, rs, pads, hs, ts = refs
     steps = LANES // REACH
     near = lax.broadcasted_iota(jnp.int32, (REACH, LANES), 0)
     lane = lax.broadcasted_iota(jnp.int32, (REACH, LANES), 1)
@@ -191,10 +201,13 @@
         ms[pl.ds(b * span, span), :] = (
             in_ref[mine, held : 2 * held, :].astype(jnp.float32).reshape(span, LANES)
         )
+    base = taps_ref.shape[1] - 2 * part
+    for i in range(count):
         for s in range(blocks):
-            high = in_ref[b * blocks + s, 2 * held : 2 * held + part, :].astype(jnp.float32)
-            low = in_ref[b * blocks + s, 2 * held + part :, :].astype(jnp.float32)
-            fs[pl.ds(s * held + b * part, part), :] = high + low
+            p = (first + i) * blocks + s
+            high = taps_ref[p, base : base + part, :].astype(jnp.float32)
+            low = taps_ref[p, base + part :, :].astype(jnp.float32)
+            fs[pl.ds(s * held + i * part, part), :] = high + low
     pads[...] = jnp.zeros_like(pads)
 
     def at(u, q, b):
@@ -280,39 +293,52 @@
 
     lax.fori_loop(0, held // unroll, several, 0)
     out_ref[:, :held, :] = cs[...].reshape(peers, held, LANES).astype(jnp.bfloat16)
-    for q in range(seqs):
+    if first:
+        out_ref[: first * blocks, held:, :] = past_ref[...]
+    for i in range(count):
         for s in range(blocks):
-            out_ref[q * blocks + s, held:, :] = rs[pl.ds(s * held + q * part, part), :].astype(
-                jnp.bfloat16
-            )
-
-
-def unpack_body(groups, in_ref, gate_ref, values_ref, gate_out, values_out, filter_out):
-    peers = in_ref.shape[0]
-    part = in_ref.shape[1] // (groups + 1)
+            block = rs[pl.ds(s * held + i * part, part), :].astype(jnp.bfloat16)
+            if first:
+                out_ref[(first + i) * blocks + s, held:, :] = block
+            else:
+                sum_ref[i * blocks + s] = block
+
+
+def unpack_body(groups, early_ref, late_ref, gate_ref, values_ref, gate_out, values_out, filter_out):
+    peers = early_ref.shape[0]
+    part = gate_ref.shape[0] // (groups * peers)
+    count = early_ref.shape[1] // part
     for q in range(groups):
         rows = pl.ds(q * peers * part, peers * part)
-        carried = (
-            in_ref[:, q * part : (q + 1) * part, :].astype(jnp.float32).reshape(peers * part, LANES)
-        )
+        src, i = (early_ref, q) if q < count else (late_ref, q - count)
+        carried = src[:, i * part : (i + 1) * part, :].astype(jnp.float32)
+        carried = carried.reshape(peers * part, LANES)
         gate_out[rows, :] = (carried * values_ref[rows, :].astype(jnp.float32)).astype(jnp.bfloat16)
         values_out[rows, :] = (carried * gate_ref[rows, :].astype(jnp.float32)).astype(jnp.bfloat16)
     filter_out[...] = (
-        in_ref[:, groups * part :, :].astype(jnp.float32).reshape(peers * part, LANES)
-    )
-
-
-def correlate(arrived, seqs):
-    peers, rows, _ = arrived.shape
+        late_ref[:, (groups - count) * part :, :].astype(jnp.float32).reshape(peers * part, LANES)
+    )
+
+
+def correlate(seqs, part, first, count, *arrays):
+    peers = arrays[0].shape[0]
     blocks = peers // seqs
-    part = rows // (2 * seqs + 2)
-    held = seqs * part
+    held = count * part
     whole = pl.BlockSpec(memory_space=pltpu.VMEM)
+    if first:
+        out_shape = jax.ShapeDtypeStruct((peers, held + part, LANES), jnp.bfloat16)
+        out_specs = whole
+    else:
+        out_shape = (
+            jax.ShapeDtypeStruct((peers, held, LANES), jnp.bfloat16),
+            jax.ShapeDtypeStruct((count * blocks, part, LANES), jnp.bfloat16),
+        )
+        out_specs = (whole, whole)
     return pl.pallas_call(
-        functools.partial(correlate_body, seqs, blocks, UNROLL),
-        out_shape=jax.ShapeDtypeStruct((peers, held + part, LANES), jnp.bfloat16),
-        in_specs=[whole],
-        out_specs=whole,
+        functools.partial(correlate_body, seqs, blocks, UNROLL, part, first, count),
+        out_shape=out_shape,
+        in_specs=[whole] * len(arrays),
+        out_specs=out_specs,
         scratch_shapes=[
             pltpu.VMEM((peers * held, LANES), jnp.float32),
             pltpu.VMEM((peers * held, LANES), jnp.float32),
@@ -324,9 +350,15 @@
             pltpu.VMEM((UNROLL, 2 * REACH, blocks * LANES), jnp.bfloat16),
         ],
         cost_estimate=pl.CostEstimate(
-            flops=6 * held * LANES * blocks * LANES * peers, bytes_accessed=4 * arrived.size, transcendentals=0
+            flops=60 * held * LANES * blocks * LANES * peers,
+            bytes_accessed=4 * arrays[0].size,
+            transcendentals=0,
         ),
-    )(arrived)
+    )(*arrays)
+
+
+def exchange(array):
+    return lax.all_to_all(array, ("dp", "seq"), split_axis=0, concat_axis=0, tiled=True)
 
 
 def direct_shards(gate_in, values_in, out_grad, filter_taps):
@@ -334,24 +366,32 @@
     peers = groups * lax.axis_size("seq")
     channels = gate_in.shape[1]
     part = channels // (groups * peers)
+    half = groups // 2
     whole = pl.BlockSpec(memory_space=pltpu.VMEM)
     own = lax.axis_index("dp").astype(jnp.int32).reshape(1)
-    packed = pl.pallas_call(
-        functools.partial(pack_body, groups, peers),
-        out_shape=jax.ShapeDtypeStruct((peers, (2 * groups + 2) * part, LANES), jnp.bfloat16),
-        in_specs=[pl.BlockSpec(memory_space=pltpu.SMEM), whole, whole, whole, whole],
-        out_specs=whole,
-    )(own, gate_in[0], values_in[0], out_grad[0], filter_taps)
-    arrived = lax.all_to_all(packed, ("dp", "seq"), split_axis=0, concat_axis=0, tiled=True)
-    made = correlate(arrived, groups)
-    home = lax.all_to_all(made, ("dp", "seq"), split_axis=0, concat_axis=0, tiled=True)
+
+    def pack(first, count):
+        rows = 2 * count + (0 if first else 2)
+        return pl.pallas_call(
+            functools.partial(pack_body, groups, peers, first, count),
+            out_shape=jax.ShapeDtypeStruct((peers, rows * part, LANES), jnp.bfloat16),
+            in_specs=[pl.BlockSpec(memory_space=pltpu.SMEM), whole, whole, whole, whole],
+            out_specs=whole,
+        )(own, gate_in[0], values_in[0], out_grad[0], filter_taps)
+
+    early = exchange(pack(0, half))
+    late = exchange(pack(half, groups - half))
+    made, sums = correlate(groups, part, 0, half, early, early)
+    early_home = exchange(made)
+    made = correlate(groups, part, half, groups - half, late, early, sums)
+    late_home = exchange(made)
     wide = jax.ShapeDtypeStruct((channels, LANES), jnp.bfloat16)
     grad_gate, grad_values, grad_filter = pl.pallas_call(
         functools.partial(unpack_body, groups),
         out_shape=(wide, wide, jax.ShapeDtypeStruct((channels // groups, LANES), jnp.float32)),
-        in_specs=[whole, whole, whole],
+        in_specs=[whole] * 4,
         out_specs=(whole, whole, whole),
-    )(home, gate_in[0], values_in[0])
+    )(early_home, late_home, gate_in[0], values_in[0])
     return (grad_gate[None], grad_values[None], grad_filter)
 
 

time: 86.1 us -> 85.8 us (level)
  blocking collectives: 62.9 us -> 18.2 us
  waiting for transfers between devices: 0 us -> 27.3 us
  starting transfers between devices: 0 us -> 12.5 us
  Pallas kernels: 22.2 us -> 26.5 us
    all_to_all x2 -> x1, blocking collectives: 62.9 us -> 18.2 us  [exchange(): lax.all_to_all(array, ('dp', 'seq'), split_axis=0, concat_axis=0, tiled=T...]
    all_to_all x0 -> x3, waiting for transfers between devices: none -> 27.3 us  [exchange(): lax.all_to_all(array, ('dp', 'seq'), split_axis=0, concat_axis=0, tiled=T...]
    all_to_all x0 -> x3, starting transfers between devices: none -> 12.5 us  [exchange(): lax.all_to_all(array, ('dp', 'seq'), split_axis=0, concat_axis=0, tiled=T...]
    pallas_call x2 -> x4, Pallas kernels: 19.6 us -> 23.9 us  [the longest x2 18.6 us: correlate(): pl.pallas_call(functools.partial(correlate_body, seqs, blocks, UNROLL, pa...]
  transfers between devices with their start and end apart: 0 -> 3, of which waited for: 0 -> 3; matrix products, arithmetic and copies ran while one was open for 0% -> 0% of each run, Pallas kernels for 0% -> 25%
where the time goes in v3:
time: 85.8 us; the launch traced here: 85.2 us
  waiting for transfers between devices  27.3 us (32%)
  Pallas kernels  26.5 us (31%)
  blocking collectives  18.2 us (21%)
  starting transfers between devices  12.5 us (15%)
    all_to_all x3, waiting for transfers between devices, exchange(): lax.all_to_all(array, ('dp', 'seq'), split_axis=0, concat_axis=0, tiled=T...  27.3 us
    pallas_call x2, Pallas kernels, correlate(): pl.pallas_call(functools.partial(correlate_body, seqs, blocks, UNROLL, pa...  18.6 us
    all_to_all x1, blocking collectives, exchange(): lax.all_to_all(array, ('dp', 'seq'), split_axis=0, concat_axis=0, tiled=T...  18.2 us
    all_to_all x3, starting transfers between devices, exchange(): lax.all_to_all(array, ('dp', 'seq'), split_axis=0, concat_axis=0, tiled=T...  12.5 us
    pallas_call x2, Pallas kernels, pack(): pl.pallas_call(functools.partial(pack_body, groups, peers, first, count),...  5.28 us
    pallas_call x1, Pallas kernels, direct_shards(): pl.pallas_call(functools.partial(unpack_body, groups), out_shape=(wide, w...  2.57 us
  transfers between devices with their start and end apart: 3, of which 3 were waited for; matrix products, arithmetic and copies ran while one was open for 0% of the time, Pallas kernels for 25%

profile of v3, /device:TPU:0, one launch (start us, length us, event | category | flops | bytes accessed | tf_op | source)
XLA Modules:
  0.0 85.2 jit_solution(18209321091991627061)
XLA Ops:
  0.6 2.7 %shard_map.67 = bf16[32,96,128]{2,1,0:T(8,128)(2,1)} custom-call(s32[1]{0:T(128)} %bitcast.own_ref, bf16[2048,128]{1,0:T(8,128)(2,1)} %bitcast.6, bf16[2048,128]{1,0:T(8,128)(2,1)} %bitcast.9, bf16[2048,128]{1,0:T(8,128)(2,1)} %bitcast.12, f32[2048,128]{1,0:T(8,128)} %taps_ref.3), custom_call_target="tpu_custom_call" | custom-call | tf_op jit(solution)/shard_map/pallas_call | solution.py:375
  3.3 7.3 %all-to-all-start = ((bf16[32,96,128]{2,1,0:T(8,128)(2,1)}), bf16[32,96,128]{2,1,0:T(8,128)(2,1)S(1)}, u32[]{:S(2)}, u32[]{:S(2)}) async-start(bf16[32,96,128]{2,1,0:T(8,128)(2,1)} %shard_map.67), calls=%async_computation | async-start | bytes 1572864 | tf_op jit(solution)/shard_map/all_to_all | solution.py:361
  10.7 2.6 %shard_map.69 = bf16[32,64,128]{2,1,0:T(8,128)(2,1)} custom-call(s32[1]{0:T(128)} %bitcast.own_ref, bf16[2048,128]{1,0:T(8,128)(2,1)} %bitcast.7, bf16[2048,128]{1,0:T(8,128)(2,1)} %bitcast.10, bf16[2048,128]{1,0:T(8,128)(2,1)} %bitcast.13, f32[2048,128]{1,0:T(8,128)} %taps_ref.3), custom_call_target="tpu_custom_call" | custom-call | tf_op jit(solution)/shard_map/pallas_call | solution.py:375
  13.2 19.3 %all-to-all-done.refs_0_.refs_1_ = bf16[32,96,128]{2,1,0:T(8,128)(2,1)S(1)} async-done(((bf16[32,96,128]{2,1,0:T(8,128)(2,1)}), bf16[32,96,128]{2,1,0:T(8,128)(2,1)S(1)}, u32[]{:S(2)}, u32[]{:S(2)}) %all-to-all-start) | async-done | bytes 786464 | tf_op jit(solution)/shard_map/all_to_all | solution.py:361
  32.5 0.0 copy-start.1
  32.5 2.6 %all-to-all-start.2 = ((bf16[32,64,128]{2,1,0:T(8,128)(2,1)}), bf16[32,64,128]{2,1,0:T(8,128)(2,1)S(1)}, u32[]{:S(2)}, u32[]{:S(2)}) async-start(bf16[32,64,128]{2,1,0:T(8,128)(2,1)} %shard_map.69), calls=%async_computation.2 | async-start | bytes 1048576 | tf_op jit(solution)/shard_map/all_to_all | solution.py:361
  35.1 0.0 copy-done.1
  35.1 9.3 %shard_map.68 = (bf16[32,32,128]{2,1,0:T(8,128)(2,1)}, bf16[16,16,128]{2,1,0:T(8,128)(2,1)}) custom-call(bf16[32,96,128]{2,1,0:T(8,128)(2,1)} %copy-done.1, bf16[32,96,128]{2,1,0:T(8,128)(2,1)} %copy-done.1), custom_call_target="tpu_custom_call" | custom-call | flops 8053063680 | bytes 1572864 | tf_op jit(solution)/shard_map/pallas_call | solution.py:337
  44.5 6.9 %all-to-all-done.2.refs_0_ = bf16[32,64,128]{2,1,0:T(8,128)(2,1)S(1)} async-done(((bf16[32,64,128]{2,1,0:T(8,128)(2,1)}), bf16[32,64,128]{2,1,0:T(8,128)(2,1)S(1)}, u32[]{:S(2)}, u32[]{:S(2)}) %all-to-all-start.2) | async-done | bytes 524320 | tf_op jit(solution)/shard_map/all_to_all | solution.py:361
  51.4 0.0 copy-start.2
  51.4 2.6 %all-to-all-start.1 = ((bf16[32,32,128]{2,1,0:T(8,128)(2,1)}), bf16[32,32,128]{2,1,0:T(8,128)(2,1)S(1)}, u32[]{:S(2)}, u32[]{:S(2)}) async-start(bf16[32,32,128]{2,1,0:T(8,128)(2,1)} %get-tuple-element.8), calls=%async_computation.1 | async-start | bytes 524288 | tf_op jit(solution)/shard_map/all_to_all | solution.py:361
  54.0 0.0 copy-done.2
  54.0 9.3 %shard_map.70 = bf16[32,48,128]{2,1,0:T(8,128)(2,1)} custom-call(bf16[32,64,128]{2,1,0:T(8,128)(2,1)} %copy-done.2, bf16[32,96,128]{2,1,0:T(8,128)(2,1)} %copy-done.1, bf16[16,16,128]{2,1,0:T(8,128)(2,1)} %get-tuple-element.9.refs_2_), custom_call_target="tpu_custom_call" | custom-call | flops 8053063680 | bytes 1048576 | tf_op jit(solution)/shard_map/pallas_call | solution.py:337
  63.2 1.1 %all-to-all-done.1.early_ref = bf16[32,32,128]{2,1,0:T(8,128)(2,1)S(1)} async-done(((bf16[32,32,128]{2,1,0:T(8,128)(2,1)}), bf16[32,32,128]{2,1,0:T(8,128)(2,1)S(1)}, u32[]{:S(2)}, u32[]{:S(2)}) %all-to-all-start.1) | async-done | bytes 262176 | tf_op jit(solution)/shard_map/all_to_all | solution.py:361
  64.4 0.0 copy-start
  64.4 18.2 %all_to_all.20.late_ref = bf16[32,48,128]{2,1,0:T(8,128)(2,1)} all-to-all(bf16[32,48,128]{2,1,0:T(8,128)(2,1)} %shard_map.70), channel_id=1, replica_groups=mesh['seq'=8,'dp'=4] {'dp','seq'}, dimensions={0} | all-to-all | bytes 786432 | tf_op jit(solution)/shard_map/all_to_all | solution.py:361
  82.6 0.0 copy-done
  82.6 2.6 %shard_map.71 = (bf16[2048,128]{1,0:T(8,128)(2,1)}, bf16[2048,128]{1,0:T(8,128)(2,1)}, f32[512,128]{1,0:T(8,128)}) custom-call(bf16[32,32,128]{2,1,0:T(8,128)(2,1)} %copy-done, bf16[32,48,128]{2,1,0:T(8,128)(2,1)} %all_to_all.20.late_ref, bf16[2048,128]{1,0:T(8,128)(2,1)} %bitcast.8, bf16[2048,128]{1,0:T(8,128)(2,1)} %bitcast.11), custom_call_target="tpu_custom_call" | custom-call | tf_op jit(solution)/shard_map/pallas_call | solution.py:389
Async XLA Ops:
  3.3 29.2 %all-to-all-start = ((bf16[32,96,128]{2,1,0:T(8,128)(2,1)}), bf16[32,96,128]{2,1,0:T(8,128)(2,1)S(1)}, u32[]{:S(2)}, u32[]{:S(2)}) async-start(bf16[32,96,128]{2,1,0:T(8,128)(2,1)} %shard_map.67), calls=%async_computation | async-start | bytes 1572864 | tf_op jit(solution)/shard_map/all_to_all | solution.py:361
  32.5 2.6 %copy-start.1 = (bf16[32,96,128]{2,1,0:T(8,128)(2,1)}, bf16[32,96,128]{2,1,0:T(8,128)(2,1)S(1)}, u32[]{:S(2)}) copy-start(bf16[32,96,128]{2,1,0:T(8,128)(2,1)S(1)} %all-to-all-done.refs_0_.refs_1_) | copy-start | bytes 2359300
  32.5 18.8 %all-to-all-start.2 = ((bf16[32,64,128]{2,1,0:T(8,128)(2,1)}), bf16[32,64,128]{2,1,0:T(8,128)(2,1)S(1)}, u32[]{:S(2)}, u32[]{:S(2)}) async-start(bf16[32,64,128]{2,1,0:T(8,128)(2,1)} %shard_map.69), calls=%async_computation.2 | async-start | bytes 1048576 | tf_op jit(solution)/shard_map/all_to_all | solution.py:361
  51.4 2.6 %copy-start.2 = (bf16[32,64,128]{2,1,0:T(8,128)(2,1)}, bf16[32,64,128]{2,1,0:T(8,128)(2,1)S(1)}, u32[]{:S(2)}) copy-start(bf16[32,64,128]{2,1,0:T(8,128)(2,1)S(1)} %all-to-all-done.2.refs_0_) | copy-start | bytes 1572868
  51.4 13.0 %all-to-all-start.1 = ((bf16[32,32,128]{2,1,0:T(8,128)(2,1)}), bf16[32,32,128]{2,1,0:T(8,128)(2,1)S(1)}, u32[]{:S(2)}, u32[]{:S(2)}) async-start(bf16[32,32,128]{2,1,0:T(8,128)(2,1)} %get-tuple-element.8), calls=%async_computation.1 | async-start | bytes 524288 | tf_op jit(solution)/shard_map/all_to_all | solution.py:361
  64.4 18.2 %copy-start = (bf16[32,32,128]{2,1,0:T(8,128)(2,1)}, bf16[32,32,128]{2,1,0:T(8,128)(2,1)S(1)}, u32[]{:S(2)}) copy-start(bf16[32,32,128]{2,1,0:T(8,128)(2,1)S(1)} %all-to-all-done.1.early_ref) | copy-start | bytes 786436

commit v4 on v2

--- a/solution.py
+++ b/solution.py
@@ -151,25 +151,55 @@
     return (grad_gate, grad_values, grad_filter)
 
 
-def pack_body(groups, peers, own_ref, gate_ref, values_ref, grad_ref, taps_ref, out_ref):
-    part = out_ref.shape[1] // (2 * groups + 2)
-    half = groups * part
-    for q in range(groups):
-        rows = pl.ds(q * peers * part, peers * part)
-        mixed = gate_ref[rows, :].astype(jnp.float32) * values_ref[rows, :].astype(jnp.float32)
-        out_ref[:, q * part : (q + 1) * part, :] = grad_ref[rows, :].reshape(peers, part, LANES)
-        out_ref[:, half + q * part : half + (q + 1) * part, :] = mixed.astype(jnp.bfloat16).reshape(
-            peers, part, LANES
+def pack_body(
+    groups, own_ref, gate_ref, values_ref, grad_ref, taps_ref, out_ref,
+    gate, values, grad, taps, mixed, split, in_sems, out_sems,
+):
+    part = grad.shape[2]
+
+    def sent(buffer, block, sem):
+        rows = pl.ds(block * part, part)
+        return pltpu.make_async_copy(buffer, out_ref.at[:, rows, :], out_sems.at[sem])
+
+    loads = {}
+    for q in range(groups):
+        loads["grad", q] = pltpu.make_async_copy(grad_ref.at[q], grad.at[q], in_sems.at[q])
+    for q in range(groups):
+        loads["gate", q] = pltpu.make_async_copy(
+            gate_ref.at[q], gate.at[q], in_sems.at[groups + 2 * q]
         )
-    first = pl.multiple_of(own_ref[0] * (peers * part), peers * part)
-    taps = taps_ref[pl.ds(first, peers * part), :]
-    high = taps.astype(jnp.bfloat16)
-    low = (taps - high.astype(jnp.float32)).astype(jnp.bfloat16)
-    out_ref[:, 2 * half : 2 * half + part, :] = high.reshape(peers, part, LANES)
-    out_ref[:, 2 * half + part :, :] = low.reshape(peers, part, LANES)
-
-
-def correlate_body(seqs, blocks, unroll, in_ref, out_ref, gs, ms, fs, cs, rs, pads, hs, ts):
+        loads["values", q] = pltpu.make_async_copy(
+            values_ref.at[q], values.at[q], in_sems.at[groups + 2 * q + 1]
+        )
+    loads["taps", 0] = pltpu.make_async_copy(
+        taps_ref.at[own_ref[0]], taps, in_sems.at[3 * groups]
+    )
+    for copy in loads.values():
+        copy.start()
+    sends = []
+    for q in range(groups):
+        loads["grad", q].wait()
+        sends.append(sent(grad.at[q], q, q))
+        sends[-1].start()
+    for q in range(groups):
+        loads["gate", q].wait()
+        loads["values", q].wait()
+        product = gate[q].astype(jnp.float32) * values[q].astype(jnp.float32)
+        mixed[q] = product.astype(jnp.bfloat16)
+        sends.append(sent(mixed.at[q], groups + q, groups + q))
+        sends[-1].start()
+    loads["taps", 0].wait()
+    high = taps[...].astype(jnp.bfloat16)
+    split[0] = high
+    split[1] = (taps[...] - high.astype(jnp.float32)).astype(jnp.bfloat16)
+    for i in range(2):
+        sends.append(sent(split.at[i], 2 * groups + i, 2 * groups + i))
+        sends[-1].start()
+    for copy in sends:
+        copy.wait()
+
+
+def correlate_body(seqs, blocks, unroll, in_ref, out_ref, gs, ms, fs, cs, rs, pads, hs0, ts0, tn0, hs1, ts1, tn1):
     peers = seqs * blocks
     part = in_ref.shape[1] // (2 * seqs + 2)
     held = seqs * part
@@ -180,6 +210,7 @@
     ours = lax.broadcasted_iota(jnp.int32, (peers, LANES), 1) // REACH
     inside = lane + REACH - 1 - near < LANES
     ahead = lane >= near
+    deep = lax.broadcasted_iota(jnp.int32, (blocks, LANES), 0)
     thin = lax.broadcasted_iota(jnp.int32, (blocks, LANES), 1)
     across = (((1,), (1,)), ((), ()))
     span = blocks * held
@@ -200,23 +231,23 @@
     def at(u, q, b):
         return ((u * steps + q) * seqs + b) * 2 * blocks
 
-    def several(i, carry):
-        lot = [(u, i * unroll + u) for u in range(unroll)]
-        for u, c in lot:
-            for b in range(seqs):
-                pads[pl.ds(at(u, 0, b), blocks), :] = gs[pl.ds(b * span + c, blocks, stride=held), :]
-        turned = []
-        for u, c in lot:
+    def turn_over(group, tn):
+        for u in range(unroll):
+            c = group * unroll + u
             mixed = ms[pl.ds(c, peers, stride=held), :]
             mixed = jnp.concatenate(
                 [jnp.where(ours == q, mixed, 0.0).astype(jnp.bfloat16) for q in range(steps)], axis=0
             )
-            turned.append(
-                lax.dot_general(flip, mixed, across, preferred_element_type=jnp.float32).astype(
-                    jnp.bfloat16
-                )
-            )
-        for u, c in lot:
+            tn[u] = lax.dot_general(
+                flip, mixed, across, preferred_element_type=jnp.float32
+            ).astype(jnp.bfloat16)
+
+    def build(group, hs, ts):
+        for u in range(unroll):
+            c = group * unroll + u
+            for b in range(seqs):
+                pads[pl.ds(at(u, 0, b), blocks), :] = gs[pl.ds(b * span + c, blocks, stride=held), :]
+        for u in range(unroll):
             for q in range(1, steps):
                 for b in range(seqs):
                     here = pads[pl.ds(at(u, 0, b), blocks), :]
@@ -224,7 +255,8 @@
                     pads[pl.ds(at(u, q, b), blocks), :] = pltpu.roll(
                         jnp.where(thin >= q * REACH, here, then), LANES - q * REACH, 1
                     )
-        for u, c in lot:
+        for u in range(unroll):
+            c = group * unroll + u
             taps = fs[pl.ds(c, blocks, stride=held), :]
             before = jnp.zeros((REACH, LANES), jnp.float32)
             for k in range(blocks):
@@ -238,18 +270,33 @@
                 block = jnp.where(ahead, turn, before)
                 before = turn
                 top = block.astype(jnp.bfloat16)
-                ts[u, :REACH, k * LANES : (k + 1) * LANES] = top
-                ts[u, REACH:, k * LANES : (k + 1) * LANES] = (
-                    block - top.astype(jnp.float32)
-                ).astype(jnp.bfloat16)
-        for u, c in lot:
+                ts[u, k, :REACH, :] = top
+                ts[u, k, REACH:, :] = (block - top.astype(jnp.float32)).astype(jnp.bfloat16)
+        for u in range(unroll):
             for q in range(steps):
                 for k in range(blocks):
-                    hs[u, q * peers : (q + 1) * peers, k * LANES : (k + 1) * LANES] = jnp.concatenate(
+                    hs[u, k, q * peers : (q + 1) * peers, :] = jnp.concatenate(
                         [pads[pl.ds(at(u, q, b) + k, blocks), :] for b in range(seqs)], axis=0
                     ).astype(jnp.bfloat16)
-        for u, c in lot:
-            gram = jnp.dot(turned[u], hs[u], preferred_element_type=jnp.float32)
+
+    def joined(ref, u):
+        return jnp.concatenate([ref[u, k] for k in range(blocks)], axis=1)
+
+    def merged(parts):
+        gap = 1
+        while len(parts) > 1:
+            keep = deep & gap == 0
+            parts = [
+                jnp.where(keep, x, y) + pltpu.roll(jnp.where(keep, y, x), gap, 0)
+                for x, y in zip(parts[0::2], parts[1::2])
+            ]
+            gap *= 2
+        return parts[0]
+
+    def multiply(group, hs, ts, tn):
+        for u in range(unroll):
+            c = group * unroll + u
+            gram = jnp.dot(tn[u], joined(hs, u), preferred_element_type=jnp.float32)
             later = jnp.zeros((REACH, LANES), jnp.float32)
             sums = []
             for k in reversed(range(blocks)):
@@ -260,11 +307,15 @@
                     stride=1,
                     stride_axis=0,
                 )
-                sums.append(jnp.sum(jnp.where(inside, turn, later), axis=0, keepdims=True))
+                picked = jnp.where(inside, turn, later)
+                sums.append(sum(picked[i : i + blocks] for i in range(0, REACH, blocks)))
                 later = turn
-            rs[pl.ds(c, blocks, stride=held), :] = jnp.concatenate(sums[::-1], axis=0)
-        for u, c in lot:
-            short = lax.dot_general(hs[u], ts[u], across, preferred_element_type=jnp.float32)
+            rs[pl.ds(c, blocks, stride=held), :] = merged(sums[::-1])
+        for u in range(unroll):
+            c = group * unroll + u
+            short = lax.dot_general(
+                joined(hs, u), joined(ts, u), across, preferred_element_type=jnp.float32
+            )
             short = jnp.concatenate(
                 [short, jnp.zeros((steps * peers, LANES - 2 * REACH), jnp.float32)], axis=1
             )
@@ -276,9 +327,22 @@
                 both = both + (pltpu.roll(mine, back * REACH, 1) if back else mine)
                 carried = both if carried is None else jnp.where(ours == q, both, carried)
             cs[pl.ds(c, peers, stride=held), :] = carried
+
+    total = held // unroll
+    turn_over(0, tn0)
+    build(0, hs0, ts0)
+
+    def twice(i, carry):
+        turn_over(2 * i + 1, tn1)
+        multiply(2 * i, hs0, ts0, tn0)
+        build(2 * i + 1, hs1, ts1)
+        after = jnp.minimum(2 * i + 2, total - 1)
+        turn_over(after, tn0)
+        multiply(2 * i + 1, hs1, ts1, tn1)
+        build(after, hs0, ts0)
         return carry
 
-    lax.fori_loop(0, held // unroll, several, 0)
+    lax.fori_loop(0, total // 2, twice, 0)
     out_ref[:, :held, :] = cs[...].reshape(peers, held, LANES).astype(jnp.bfloat16)
     for q in range(seqs):
         for s in range(blocks):
@@ -287,19 +351,43 @@
             )
 
 
-def unpack_body(groups, in_ref, gate_ref, values_ref, gate_out, values_out, filter_out):
-    peers = in_ref.shape[0]
-    part = in_ref.shape[1] // (groups + 1)
-    for q in range(groups):
-        rows = pl.ds(q * peers * part, peers * part)
-        carried = (
-            in_ref[:, q * part : (q + 1) * part, :].astype(jnp.float32).reshape(peers * part, LANES)
+def unpack_body(
+    groups, in_ref, gate_ref, values_ref, gate_out, values_out, filter_out,
+    home, gate, values, gate_made, values_made, sums, in_sems, out_sems,
+):
+    part = home.shape[2]
+    loads, sends = [], []
+    for q in range(groups):
+        rows = pl.ds(q * part, part)
+        loads.append(
+            [
+                pltpu.make_async_copy(in_ref.at[:, rows, :], home.at[q], in_sems.at[3 * q]),
+                pltpu.make_async_copy(gate_ref.at[q], gate.at[q], in_sems.at[3 * q + 1]),
+                pltpu.make_async_copy(values_ref.at[q], values.at[q], in_sems.at[3 * q + 2]),
+            ]
         )
-        gate_out[rows, :] = (carried * values_ref[rows, :].astype(jnp.float32)).astype(jnp.bfloat16)
-        values_out[rows, :] = (carried * gate_ref[rows, :].astype(jnp.float32)).astype(jnp.bfloat16)
-    filter_out[...] = (
-        in_ref[:, groups * part :, :].astype(jnp.float32).reshape(peers * part, LANES)
-    )
+    tail = pltpu.make_async_copy(
+        in_ref.at[:, pl.ds(groups * part, part), :], home.at[groups], in_sems.at[3 * groups]
+    )
+    for copies in loads:
+        for copy in copies:
+            copy.start()
+    tail.start()
+    for q in range(groups):
+        for copy in loads[q]:
+            copy.wait()
+        carried = home[q].astype(jnp.float32)
+        gate_made[q] = (carried * values[q].astype(jnp.float32)).astype(jnp.bfloat16)
+        values_made[q] = (carried * gate[q].astype(jnp.float32)).astype(jnp.bfloat16)
+        for i, (made, out) in enumerate(((gate_made, gate_out), (values_made, values_out))):
+            sends.append(pltpu.make_async_copy(made.at[q], out.at[q], out_sems.at[2 * q + i]))
+            sends[-1].start()
+    tail.wait()
+    sums[...] = home[groups].astype(jnp.float32)
+    sends.append(pltpu.make_async_copy(sums, filter_out, out_sems.at[2 * groups]))
+    sends[-1].start()
+    for copy in sends:
+        copy.wait()
 
 
 def correlate(arrived, seqs):
@@ -320,8 +408,12 @@
             pltpu.VMEM((peers * held, LANES), jnp.float32),
             pltpu.VMEM((blocks * held, LANES), jnp.float32),
             pltpu.VMEM((UNROLL * (LANES // REACH) * 2 * peers, LANES), jnp.float32),
-            pltpu.VMEM((UNROLL, LANES // REACH * peers, blocks * LANES), jnp.bfloat16),
-            pltpu.VMEM((UNROLL, 2 * REACH, blocks * LANES), jnp.bfloat16),
+            *[
+                pltpu.VMEM((UNROLL, blocks, LANES // REACH * peers, LANES), jnp.bfloat16),
+                pltpu.VMEM((UNROLL, blocks, 2 * REACH, LANES), jnp.bfloat16),
+                pltpu.VMEM((UNROLL, REACH, LANES // REACH * peers), jnp.bfloat16),
+            ]
+            * 2,
         ],
         cost_estimate=pl.CostEstimate(
             flops=6 * held * LANES * blocks * LANES * peers, bytes_accessed=4 * arrived.size, transcendentals=0
@@ -334,25 +426,53 @@
     peers = groups * lax.axis_size("seq")
     channels = gate_in.shape[1]
     part = channels // (groups * peers)
-    whole = pl.BlockSpec(memory_space=pltpu.VMEM)
+    shape = (groups, peers, part, LANES)
+    gate, values, grad = (array.reshape(shape) for array in (gate_in, values_in, out_grad))
+    taps = filter_taps.reshape(shape)
     own = lax.axis_index("dp").astype(jnp.int32).reshape(1)
+    far = pl.BlockSpec(memory_space=pl.ANY)
+    half = pltpu.VMEM(shape, jnp.bfloat16)
     packed = pl.pallas_call(
-        functools.partial(pack_body, groups, peers),
+        functools.partial(pack_body, groups),
         out_shape=jax.ShapeDtypeStruct((peers, (2 * groups + 2) * part, LANES), jnp.bfloat16),
-        in_specs=[pl.BlockSpec(memory_space=pltpu.SMEM), whole, whole, whole, whole],
-        out_specs=whole,
-    )(own, gate_in[0], values_in[0], out_grad[0], filter_taps)
+        in_specs=[pl.BlockSpec(memory_space=pltpu.SMEM), far, far, far, far],
+        out_specs=far,
+        scratch_shapes=[
+            half,
+            half,
+            half,
+            pltpu.VMEM(shape[1:], jnp.float32),
+            half,
+            pltpu.VMEM((2,) + shape[1:], jnp.bfloat16),
+            pltpu.SemaphoreType.DMA((3 * groups + 1,)),
+            pltpu.SemaphoreType.DMA((2 * groups + 2,)),
+        ],
+    )(own, gate, values, grad, taps)
     arrived = lax.all_to_all(packed, ("dp", "seq"), split_axis=0, concat_axis=0, tiled=True)
     made = correlate(arrived, groups)
     home = lax.all_to_all(made, ("dp", "seq"), split_axis=0, concat_axis=0, tiled=True)
-    wide = jax.ShapeDtypeStruct((channels, LANES), jnp.bfloat16)
+    wide = jax.ShapeDtypeStruct(shape, jnp.bfloat16)
     grad_gate, grad_values, grad_filter = pl.pallas_call(
         functools.partial(unpack_body, groups),
-        out_shape=(wide, wide, jax.ShapeDtypeStruct((channels // groups, LANES), jnp.float32)),
-        in_specs=[whole, whole, whole],
-        out_specs=(whole, whole, whole),
-    )(home, gate_in[0], values_in[0])
-    return (grad_gate[None], grad_values[None], grad_filter)
+        out_shape=(wide, wide, jax.ShapeDtypeStruct(shape[1:], jnp.float32)),
+        in_specs=[far, far, far],
+        out_specs=(far, far, far),
+        scratch_shapes=[
+            pltpu.VMEM((groups + 1,) + shape[1:], jnp.bfloat16),
+            half,
+            half,
+            half,
+            half,
+            pltpu.VMEM(shape[1:], jnp.float32),
+            pltpu.SemaphoreType.DMA((3 * groups + 1,)),
+            pltpu.SemaphoreType.DMA((2 * groups + 1,)),
+        ],
+    )(home, gate, values)
+    return (
+        grad_gate.reshape(gate_in.shape),
+        grad_values.reshape(gate_in.shape),
+        grad_filter.reshape(channels // groups, LANES),
+    )
 
 
 def shards(gate_in, values_in, out_grad, filter_taps):

time: 86.1 us -> 83.3 us (0.967)
  Pallas kernels: 22.2 us -> 19.4 us
    pallas_call x1, Pallas kernels: 16.6 us -> 14.4 us  [correlate(): pl.pallas_call(functools.partial(correlate_body, seqs, blocks, UNROLL), o...]
where the time goes in v4:
time: 83.3 us; the launch traced here: 82.9 us
  blocking collectives  62.9 us (76%)
  Pallas kernels  19.4 us (23%)
    all_to_all x1, blocking collectives, direct_shards(): lax.all_to_all(packed, ('dp', 'seq'), split_axis=0, concat_axis=0, tiled=...  40.5 us
    all_to_all x1, blocking collectives, direct_shards(): lax.all_to_all(made, ('dp', 'seq'), split_axis=0, concat_axis=0, tiled=True)  22.4 us
    pallas_call x1, Pallas kernels, correlate(): pl.pallas_call(functools.partial(correlate_body, seqs, blocks, UNROLL), o...  14.4 us
    pallas_call x1, Pallas kernels, direct_shards(): pl.pallas_call(functools.partial(pack_body, groups), out_shape=jax.ShapeD...  2.53 us
    pallas_call x1, Pallas kernels, direct_shards(): pl.pallas_call(functools.partial(unpack_body, groups), out_shape=(wide, w...  2.46 us

profile of v4, /device:TPU:0, one launch (start us, length us, event | category | flops | bytes accessed | tf_op | source)
XLA Modules:
  0.0 82.9 jit_solution(8150108678186896465)
XLA Ops:
  0.6 2.5 %shard_map.67 = bf16[32,160,128]{2,1,0:T(8,128)(2,1)} custom-call(s32[1]{0:T(128)} %bitcast.own_ref, bf16[4,32,16,128]{3,2,1,0:T(8,128)(2,1)} %bitcast.8, bf16[4,32,16,128]{3,2,1,0:T(8,128)(2,1)} %bitcast.10, bf16[4,32,16,128]{3,2,1,0:T(8,128)(2,1)} %bitcast.13, f32[4,32,16,128]{3,2,1,0:T(8,128)} %bitcast.12), custom_call_target="tpu_custom_call" | custom-call | tf_op jit(solution)/shard_map/pallas_call | solution.py:435
  3.2 40.5 %all_to_all.10.in_ref = bf16[32,160,128]{2,1,0:T(8,128)(2,1)} all-to-all(bf16[32,160,128]{2,1,0:T(8,128)(2,1)} %shard_map.67), channel_id=1, replica_groups=mesh['seq'=8,'dp'=4] {'dp','seq'}, dimensions={0} | all-to-all | bytes 2621440 | tf_op jit(solution)/shard_map/all_to_all | solution.py:451
  43.7 14.4 %shard_map.68 = bf16[32,80,128]{2,1,0:T(8,128)(2,1)} custom-call(bf16[32,160,128]{2,1,0:T(8,128)(2,1)} %all_to_all.10.in_ref), custom_call_target="tpu_custom_call" | custom-call | flops 1610612736 | bytes 2621440 | tf_op jit(solution)/shard_map/pallas_call | solution.py:399
  58.1 22.4 %all_to_all.11.in_ref = bf16[32,80,128]{2,1,0:T(8,128)(2,1)} all-to-all(bf16[32,80,128]{2,1,0:T(8,128)(2,1)} %shard_map.68), channel_id=1, replica_groups=mesh['seq'=8,'dp'=4] {'dp','seq'}, dimensions={0} | all-to-all | bytes 1310720 | tf_op jit(solution)/shard_map/all_to_all | solution.py:453
  80.5 2.5 %shard_map.69 = (bf16[4,32,16,128]{3,2,1,0:T(8,128)(2,1)}, bf16[4,32,16,128]{3,2,1,0:T(8,128)(2,1)}, f32[32,16,128]{2,1,0:T(8,128)}) custom-call(bf16[32,80,128]{2,1,0:T(8,128)(2,1)} %all_to_all.11.in_ref, bf16[4,32,16,128]{3,2,1,0:T(8,128)(2,1)} %bitcast.9, bf16[4,32,16,128]{3,2,1,0:T(8,128)(2,1)} %bitcast.11), custom_call_target="tpu_custom_call" | custom-call | tf_op jit(solution)/shard_map/pallas_call | solution.py:455

commit v5 on v4

--- a/solution.py
+++ b/solution.py
@@ -152,51 +152,37 @@
 
 
 def pack_body(
-    groups, own_ref, gate_ref, values_ref, grad_ref, taps_ref, out_ref,
-    gate, values, grad, taps, mixed, split, in_sems, out_sems,
+    groups, own_ref, gate_ref, values_ref, grad_ref, taps_ref, out_ref, gate, values, taps, sems
 ):
-    part = grad.shape[2]
-
-    def sent(buffer, block, sem):
-        rows = pl.ds(block * part, part)
-        return pltpu.make_async_copy(buffer, out_ref.at[:, rows, :], out_sems.at[sem])
-
+    part = gate.shape[2]
     loads = {}
+    loads["taps", 0] = pltpu.make_async_copy(
+        taps_ref.at[own_ref[0]], taps, sems.at[3 * groups]
+    )
     for q in range(groups):
-        loads["grad", q] = pltpu.make_async_copy(grad_ref.at[q], grad.at[q], in_sems.at[q])
+        loads["gate", q] = pltpu.make_async_copy(gate_ref.at[q], gate.at[q], sems.at[2 * q])
+        loads["values", q] = pltpu.make_async_copy(
+            values_ref.at[q], values.at[q], sems.at[2 * q + 1]
+        )
     for q in range(groups):
-        loads["gate", q] = pltpu.make_async_copy(
-            gate_ref.at[q], gate.at[q], in_sems.at[groups + 2 * q]
+        loads["grad", q] = pltpu.make_async_copy(
+            grad_ref.at[q], out_ref.at[:, pl.ds(q * part, part), :], sems.at[2 * groups + q]
         )
-        loads["values", q] = pltpu.make_async_copy(
-            values_ref.at[q], values.at[q], in_sems.at[groups + 2 * q + 1]
-        )
-    loads["taps", 0] = pltpu.make_async_copy(
-        taps_ref.at[own_ref[0]], taps, in_sems.at[3 * groups]
-    )
     for copy in loads.values():
         copy.start()
-    sends = []
-    for q in range(groups):
-        loads["grad", q].wait()
-        sends.append(sent(grad.at[q], q, q))
-        sends[-1].start()
+    loads["taps", 0].wait()
+    high = taps[...].astype(jnp.bfloat16)
+    out_ref[:, 2 * groups * part : (2 * groups + 1) * part, :] = high
+    out_ref[:, (2 * groups + 1) * part :, :] = (taps[...] - high.astype(jnp.float32)).astype(
+        jnp.bfloat16
+    )
     for q in range(groups):
         loads["gate", q].wait()
         loads["values", q].wait()
         product = gate[q].astype(jnp.float32) * values[q].astype(jnp.float32)
-        mixed[q] = product.astype(jnp.bfloat16)
-        sends.append(sent(mixed.at[q], groups + q, groups + q))
-        sends[-1].start()
-    loads["taps", 0].wait()
-    high = taps[...].astype(jnp.bfloat16)
-    split[0] = high
-    split[1] = (taps[...] - high.astype(jnp.float32)).astype(jnp.bfloat16)
-    for i in range(2):
-        sends.append(sent(split.at[i], 2 * groups + i, 2 * groups + i))
-        sends[-1].start()
-    for copy in sends:
-        copy.wait()
+        out_ref[:, (groups + q) * part : (groups + q + 1) * part, :] = product.astype(jnp.bfloat16)
+    for q in range(groups):
+        loads["grad", q].wait()
 
 
 def correlate_body(seqs, blocks, unroll, in_ref, out_ref, gs, ms, fs, cs, rs, pads, hs0, ts0, tn0, hs1, ts1, tn1):
@@ -352,40 +338,19 @@
 
 
 def unpack_body(
-    groups, in_ref, gate_ref, values_ref, gate_out, values_out, filter_out,
-    home, gate, values, gate_made, values_made, sums, in_sems, out_sems,
+    groups, home, gate, values, gate_out, values_out, filter_out, gate_made, values_made, sums, sems
 ):
-    part = home.shape[2]
-    loads, sends = [], []
+    part = gate.shape[2]
+    sums[...] = home[:, groups * part :, :].astype(jnp.float32)
+    sends = [pltpu.make_async_copy(sums, filter_out, sems.at[2 * groups])]
+    sends[-1].start()
     for q in range(groups):
-        rows = pl.ds(q * part, part)
-        loads.append(
-            [
-                pltpu.make_async_copy(in_ref.at[:, rows, :], home.at[q], in_sems.at[3 * q]),
-                pltpu.make_async_copy(gate_ref.at[q], gate.at[q], in_sems.at[3 * q + 1]),
-                pltpu.make_async_copy(values_ref.at[q], values.at[q], in_sems.at[3 * q + 2]),
-            ]
-        )
-    tail = pltpu.make_async_copy(
-        in_ref.at[:, pl.ds(groups * part, part), :], home.at[groups], in_sems.at[3 * groups]
-    )
-    for copies in loads:
-        for copy in copies:
-            copy.start()
-    tail.start()
-    for q in range(groups):
-        for copy in loads[q]:
-            copy.wait()
-        carried = home[q].astype(jnp.float32)
+        carried = home[:, q * part : (q + 1) * part, :].astype(jnp.float32)
         gate_made[q] = (carried * values[q].astype(jnp.float32)).astype(jnp.bfloat16)
         values_made[q] = (carried * gate[q].astype(jnp.float32)).astype(jnp.bfloat16)
         for i, (made, out) in enumerate(((gate_made, gate_out), (values_made, values_out))):
-            sends.append(pltpu.make_async_copy(made.at[q], out.at[q], out_sems.at[2 * q + i]))
+            sends.append(pltpu.make_async_copy(made.at[q], out.at[q], sems.at[2 * q + i]))
             sends[-1].start()
-    tail.wait()
-    sums[...] = home[groups].astype(jnp.float32)
-    sends.append(pltpu.make_async_copy(sums, filter_out, out_sems.at[2 * groups]))
-    sends[-1].start()
     for copy in sends:
         copy.wait()
 
@@ -421,6 +386,10 @@
     )(arrived)
 
 
+def exchange(array):
+    return lax.all_to_all(array, ("dp", "seq"), split_axis=0, concat_axis=0, tiled=True)
+
+
 def direct_shards(gate_in, values_in, out_grad, filter_taps):
     groups = lax.axis_size("dp")
     peers = groups * lax.axis_size("seq")
@@ -436,38 +405,32 @@
         functools.partial(pack_body, groups),
         out_shape=jax.ShapeDtypeStruct((peers, (2 * groups + 2) * part, LANES), jnp.bfloat16),
         in_specs=[pl.BlockSpec(memory_space=pltpu.SMEM), far, far, far, far],
-        out_specs=far,
+        out_specs=pl.BlockSpec(memory_space=pltpu.VMEM),
         scratch_shapes=[
-            half,
-            half,
-            half,
-            pltpu.VMEM(shape[1:], jnp.float32),
-            half,
-            pltpu.VMEM((2,) + shape[1:], jnp.bfloat16),
-            pltpu.SemaphoreType.DMA((3 * groups + 1,)),
-            pltpu.SemaphoreType.DMA((2 * groups + 2,)),
-        ],
-    )(own, gate, values, grad, taps)
-    arrived = lax.all_to_all(packed, ("dp", "seq"), split_axis=0, concat_axis=0, tiled=True)
-    made = correlate(arrived, groups)
-    home = lax.all_to_all(made, ("dp", "seq"), split_axis=0, concat_axis=0, tiled=True)
-    wide = jax.ShapeDtypeStruct(shape, jnp.bfloat16)
-    grad_gate, grad_values, grad_filter = pl.pallas_call(
-        functools.partial(unpack_body, groups),
-        out_shape=(wide, wide, jax.ShapeDtypeStruct(shape[1:], jnp.float32)),
-        in_specs=[far, far, far],
-        out_specs=(far, far, far),
-        scratch_shapes=[
-            pltpu.VMEM((groups + 1,) + shape[1:], jnp.bfloat16),
-            half,
-            half,
             half,
             half,
             pltpu.VMEM(shape[1:], jnp.float32),
             pltpu.SemaphoreType.DMA((3 * groups + 1,)),
+        ],
+    )(own, gate, values, grad, taps)
+    near = functools.partial(pltpu.with_memory_space_constraint, memory_space=pltpu.VMEM)
+    arrived = near(exchange(packed))
+    made = correlate(arrived, groups)
+    home = near(exchange(made))
+    wide = jax.ShapeDtypeStruct(shape, jnp.bfloat16)
+    local = pl.BlockSpec(memory_space=pltpu.VMEM)
+    grad_gate, grad_values, grad_filter = pl.pallas_call(
+        functools.partial(unpack_body, groups),
+        out_shape=(wide, wide, jax.ShapeDtypeStruct(shape[1:], jnp.float32)),
+        in_specs=[local, local, local],
+        out_specs=(far, far, far),
+        scratch_shapes=[
+            half,
+            half,
+            pltpu.VMEM(shape[1:], jnp.float32),
             pltpu.SemaphoreType.DMA((2 * groups + 1,)),
         ],
-    )(home, gate, values)
+    )(home, near(gate), near(values))
     return (
         grad_gate.reshape(gate_in.shape),
         grad_values.reshape(gate_in.shape),

time: 83.3 us -> 80 us (0.960)
  Pallas kernels: 19.4 us -> 16.9 us
    pallas_call x1, Pallas kernels: 2.46 us -> 1.14 us  [direct_shards(): pl.pallas_call(functools.partial(unpack_body, groups), out_shape=(wide, w...]
    pallas_call x1, Pallas kernels: 14.4 us -> 13.1 us  [correlate(): pl.pallas_call(functools.partial(correlate_body, seqs, blocks, UNROLL), o...]
where the time goes in v5:
time: 80 us; the launch traced here: 79.7 us
  blocking collectives  62.2 us (78%)
  Pallas kernels  16.9 us (21%)
    all_to_all x2, blocking collectives, exchange(): lax.all_to_all(array, ('dp', 'seq'), split_axis=0, concat_axis=0, tiled=T...  62.2 us
    pallas_call x1, Pallas kernels, correlate(): pl.pallas_call(functools.partial(correlate_body, seqs, blocks, UNROLL), o...  13.1 us
    pallas_call x1, Pallas kernels, direct_shards(): pl.pallas_call(functools.partial(pack_body, groups), out_shape=jax.ShapeD...  2.64 us

profile of v5, /device:TPU:0, one launch (start us, length us, event | category | flops | bytes accessed | tf_op | source)
XLA Modules:
  0.0 79.7 jit_solution(11288717229695327454)
XLA Ops:
  0.6 2.6 %shard_map.67 = bf16[32,160,128]{2,1,0:T(8,128)(2,1)} custom-call(s32[1]{0:T(128)} %bitcast.own_ref, bf16[4,32,16,128]{3,2,1,0:T(8,128)(2,1)} %bitcast.8, bf16[4,32,16,128]{3,2,1,0:T(8,128)(2,1)} %bitcast.10, bf16[4,32,16,128]{3,2,1,0:T(8,128)(2,1)} %bitcast.13, f32[4,32,16,128]{3,2,1,0:T(8,128)} %bitcast.12), custom_call_target="tpu_custom_call" | custom-call | tf_op jit(solution)/shard_map/pallas_call | solution.py:404
  3.3 40.4 %all_to_all.10.in_ref = bf16[32,160,128]{2,1,0:T(8,128)(2,1)S(1)} all-to-all(bf16[32,160,128]{2,1,0:T(8,128)(2,1)} %shard_map.67), channel_id=1, replica_groups=mesh['seq'=8,'dp'=4] {'dp','seq'}, dimensions={0} | all-to-all | bytes 2621440 | tf_op jit(solution)/shard_map/all_to_all | solution.py:390
  43.7 13.1 %shard_map.68 = bf16[32,80,128]{2,1,0:T(8,128)(2,1)} custom-call(bf16[32,160,128]{2,1,0:T(8,128)(2,1)S(1)} %all_to_all.10.in_ref), custom_call_target="tpu_custom_call" | custom-call | flops 1610612736 | bytes 2621440 | tf_op jit(solution)/shard_map/pallas_call | solution.py:364
  56.8 0.0 copy-start
  56.8 0.0 copy-start.1
  56.8 21.8 %all_to_all.11.home = bf16[32,80,128]{2,1,0:T(8,128)(2,1)S(1)} all-to-all(bf16[32,80,128]{2,1,0:T(8,128)(2,1)} %shard_map.68), channel_id=1, replica_groups=mesh['seq'=8,'dp'=4] {'dp','seq'}, dimensions={0} | all-to-all | bytes 1310720 | tf_op jit(solution)/shard_map/all_to_all | solution.py:390
  78.6 0.0 copy-done
  78.6 0.0 copy-done.1
  78.6 1.1 %shard_map.69 = (bf16[4,32,16,128]{3,2,1,0:T(8,128)(2,1)}, bf16[4,32,16,128]{3,2,1,0:T(8,128)(2,1)}, f32[32,16,128]{2,1,0:T(8,128)}) custom-call(bf16[32,80,128]{2,1,0:T(8,128)(2,1)S(1)} %all_to_all.11.home, bf16[4,32,16,128]{3,2,1,0:T(8,128)(2,1)S(1)} %bitcast.9, bf16[4,32,16,128]{3,2,1,0:T(8,128)(2,1)S(1)} %bitcast.11), custom_call_target="tpu_custom_call" | custom-call | tf_op jit(solution)/shard_map/pallas_call | solution.py:422
Async XLA Ops:
  56.8 21.8 %copy-start = (bf16[1,2048,128]{2,1,0:T(8,128)(2,1)S(1)}, bf16[1,2048,128]{2,1,0:T(8,128)(2,1)}, u32[]{:S(2)}) copy-start(bf16[1,2048,128]{2,1,0:T(8,128)(2,1)} %param.4) | copy-start | bytes 1572868
  56.8 21.8 %copy-start.1 = (bf16[1,2048,128]{2,1,0:T(8,128)(2,1)S(1)}, bf16[1,2048,128]{2,1,0:T(8,128)(2,1)}, u32[]{:S(2)}) copy-start(bf16[1,2048,128]{2,1,0:T(8,128)(2,1)} %param.5) | copy-start | bytes 1572868

commit v6 on v5

--- a/solution.py
+++ b/solution.py
@@ -12,6 +12,7 @@
 SUBLANES = 16
 REACH = 32
 UNROLL = 8
+EARLY = 96
 ROOM = 40 * 2**20
 
 precise = lax.Precision.HIGHEST
@@ -152,43 +153,67 @@
 
 
 def pack_body(
-    groups, own_ref, gate_ref, values_ref, grad_ref, taps_ref, out_ref, gate, values, taps, sems
+    first, count, own_ref, gate_ref, values_ref, grad_ref, taps_ref, out_ref, gate, values, taps, sems
 ):
     part = gate.shape[2]
     loads = {}
-    loads["taps", 0] = pltpu.make_async_copy(
-        taps_ref.at[own_ref[0]], taps, sems.at[3 * groups]
-    )
-    for q in range(groups):
-        loads["gate", q] = pltpu.make_async_copy(gate_ref.at[q], gate.at[q], sems.at[2 * q])
-        loads["values", q] = pltpu.make_async_copy(
-            values_ref.at[q], values.at[q], sems.at[2 * q + 1]
-        )
-    for q in range(groups):
-        loads["grad", q] = pltpu.make_async_copy(
-            grad_ref.at[q], out_ref.at[:, pl.ds(q * part, part), :], sems.at[2 * groups + q]
+    if not first:
+        loads["taps", 0] = pltpu.make_async_copy(
+            taps_ref.at[own_ref[0]], taps, sems.at[3 * count]
+        )
+    for i in range(count):
+        q = first + i
+        loads["gate", i] = pltpu.make_async_copy(gate_ref.at[q], gate.at[i], sems.at[2 * i])
+        loads["values", i] = pltpu.make_async_copy(
+            values_ref.at[q], values.at[i], sems.at[2 * i + 1]
+        )
+    for i in range(count):
+        loads["grad", i] = pltpu.make_async_copy(
+            grad_ref.at[first + i],
+            out_ref.at[:, pl.ds(i * part, part), :],
+            sems.at[2 * count + i],
         )
     for copy in loads.values():
         copy.start()
-    loads["taps", 0].wait()
-    high = taps[...].astype(jnp.bfloat16)
-    out_ref[:, 2 * groups * part : (2 * groups + 1) * part, :] = high
-    out_ref[:, (2 * groups + 1) * part :, :] = (taps[...] - high.astype(jnp.float32)).astype(
-        jnp.bfloat16
-    )
-    for q in range(groups):
-        loads["gate", q].wait()
-        loads["values", q].wait()
-        product = gate[q].astype(jnp.float32) * values[q].astype(jnp.float32)
-        out_ref[:, (groups + q) * part : (groups + q + 1) * part, :] = product.astype(jnp.bfloat16)
-    for q in range(groups):
-        loads["grad", q].wait()
-
-
-def correlate_body(seqs, blocks, unroll, in_ref, out_ref, gs, ms, fs, cs, rs, pads, hs0, ts0, tn0, hs1, ts1, tn1):
+    if not first:
+        loads["taps", 0].wait()
+        high = taps[...].astype(jnp.bfloat16)
+        out_ref[:, 2 * count * part : (2 * count + 1) * part, :] = high
+        out_ref[:, (2 * count + 1) * part :, :] = (taps[...] - high.astype(jnp.float32)).astype(
+            jnp.bfloat16
+        )
+    for i in range(count):
+        loads["gate", i].wait()
+        loads["values", i].wait()
+        product = gate[i].astype(jnp.float32) * values[i].astype(jnp.float32)
+        out_ref[:, (count + i) * part : (count + i + 1) * part, :] = product.astype(jnp.bfloat16)
+    for i in range(count):
+        loads["grad", i].wait()
+
+
+def correlate_body(seqs, blocks, unroll, part, first, count, *refs):
     peers = seqs * blocks
-    part = in_ref.shape[1] // (2 * seqs + 2)
-    held = seqs * part
+    held = count * part
+    if first:
+        in_ref, taps_ref, early_ref, early_sums_ref, out_ref, *refs = refs
+    else:
+        in_ref, out_ref, sums_ref, *refs = refs
+        taps_ref = in_ref
+    gs, ms, fs, cs, rs, pads, hs0, ts0, tn0, hs1, ts1, tn1, sems = refs
+    moves = []
+    if first:
+        moves = [
+            pltpu.make_async_copy(
+                early_ref, out_ref.at[:, pl.ds(0, first * part), :], sems.at[0]
+            ),
+            pltpu.make_async_copy(
+                early_sums_ref,
+                out_ref.at[pl.ds(0, first * blocks), pl.ds(seqs * part, part), :],
+                sems.at[1],
+            ),
+        ]
+    for move in moves:
+        move.start()
     steps = LANES // REACH
     near = lax.broadcasted_iota(jnp.int32, (REACH, LANES), 0)
     lane = lax.broadcasted_iota(jnp.int32, (REACH, LANES), 1)
@@ -208,10 +233,13 @@
         ms[pl.ds(b * span, span), :] = (
             in_ref[mine, held : 2 * held, :].astype(jnp.float32).reshape(span, LANES)
         )
+    base = taps_ref.shape[1] - 2 * part
+    for i in range(count):
         for s in range(blocks):
-            high = in_ref[b * blocks + s, 2 * held : 2 * held + part, :].astype(jnp.float32)
-            low = in_ref[b * blocks + s, 2 * held + part :, :].astype(jnp.float32)
-            fs[pl.ds(s * held + b * part, part), :] = high + low
+            p = (first + i) * blocks + s
+            high = taps_ref[p, base : base + part, :].astype(jnp.float32)
+            low = taps_ref[p, base + part :, :].astype(jnp.float32)
+            fs[pl.ds(s * held + i * part, part), :] = high + low
     pads[...] = jnp.zeros_like(pads)
 
     def at(u, q, b):
@@ -329,12 +357,18 @@
         return carry
 
     lax.fori_loop(0, total // 2, twice, 0)
-    out_ref[:, :held, :] = cs[...].reshape(peers, held, LANES).astype(jnp.bfloat16)
-    for q in range(seqs):
+    made = cs[...].reshape(peers, held, LANES).astype(jnp.bfloat16)
+    ahead_rows = first * part
+    out_ref[:, ahead_rows : ahead_rows + held, :] = made
+    for i in range(count):
         for s in range(blocks):
-            out_ref[q * blocks + s, held:, :] = rs[pl.ds(s * held + q * part, part), :].astype(
-                jnp.bfloat16
-            )
+            block = rs[pl.ds(s * held + i * part, part), :].astype(jnp.bfloat16)
+            if first:
+                out_ref[(first + i) * blocks + s, seqs * part :, :] = block
+            else:
+                sums_ref[i * blocks + s] = block
+    for move in moves:
+        move.wait()
 
 
 def unpack_body(
@@ -355,17 +389,23 @@
         copy.wait()
 
 
-def correlate(arrived, seqs):
-    peers, rows, _ = arrived.shape
+def correlate(seqs, part, first, count, *arrays):
+    peers = arrays[0].shape[0]
     blocks = peers // seqs
-    part = rows // (2 * seqs + 2)
-    held = seqs * part
+    held = count * part
     whole = pl.BlockSpec(memory_space=pltpu.VMEM)
+    if first:
+        out_shape = (jax.ShapeDtypeStruct((peers, (seqs + 1) * part, LANES), jnp.bfloat16),)
+    else:
+        out_shape = (
+            jax.ShapeDtypeStruct((peers, held, LANES), jnp.bfloat16),
+            jax.ShapeDtypeStruct((count * blocks, part, LANES), jnp.bfloat16),
+        )
     return pl.pallas_call(
-        functools.partial(correlate_body, seqs, blocks, UNROLL),
-        out_shape=jax.ShapeDtypeStruct((peers, held + part, LANES), jnp.bfloat16),
-        in_specs=[whole],
-        out_specs=whole,
+        functools.partial(correlate_body, seqs, blocks, UNROLL, part, first, count),
+        out_shape=out_shape,
+        in_specs=[whole] * min(len(arrays), 2) + [pl.BlockSpec(memory_space=pl.ANY)] * (len(arrays) - 2),
+        out_specs=(whole,) * len(out_shape),
         scratch_shapes=[
             pltpu.VMEM((peers * held, LANES), jnp.float32),
             pltpu.VMEM((peers * held, LANES), jnp.float32),
@@ -379,11 +419,14 @@
                 pltpu.VMEM((UNROLL, REACH, LANES // REACH * peers), jnp.bfloat16),
             ]
             * 2,
+            pltpu.SemaphoreType.DMA((2,)),
         ],
         cost_estimate=pl.CostEstimate(
-            flops=6 * held * LANES * blocks * LANES * peers, bytes_accessed=4 * arrived.size, transcendentals=0
+            flops=60 * held * LANES * blocks * LANES * peers,
+            bytes_accessed=4 * arrays[0].size,
+            transcendentals=0,
         ),
-    )(arrived)
+    )(*arrays)
 
 
 def exchange(array):
@@ -401,21 +444,30 @@
     own = lax.axis_index("dp").astype(jnp.int32).reshape(1)
     far = pl.BlockSpec(memory_space=pl.ANY)
     half = pltpu.VMEM(shape, jnp.bfloat16)
-    packed = pl.pallas_call(
-        functools.partial(pack_body, groups),
-        out_shape=jax.ShapeDtypeStruct((peers, (2 * groups + 2) * part, LANES), jnp.bfloat16),
-        in_specs=[pl.BlockSpec(memory_space=pltpu.SMEM), far, far, far, far],
-        out_specs=pl.BlockSpec(memory_space=pltpu.VMEM),
-        scratch_shapes=[
-            half,
-            half,
-            pltpu.VMEM(shape[1:], jnp.float32),
-            pltpu.SemaphoreType.DMA((3 * groups + 1,)),
-        ],
-    )(own, gate, values, grad, taps)
     near = functools.partial(pltpu.with_memory_space_constraint, memory_space=pltpu.VMEM)
-    arrived = near(exchange(packed))
-    made = correlate(arrived, groups)
+    early = groups * EARLY // LANES
+    late = groups - early
+
+    def pack(first, count):
+        rows = (2 * count + (0 if first else 2)) * part
+        kept = pltpu.VMEM((count,) + shape[1:], jnp.bfloat16)
+        return pl.pallas_call(
+            functools.partial(pack_body, first, count),
+            out_shape=jax.ShapeDtypeStruct((peers, rows, LANES), jnp.bfloat16),
+            in_specs=[pl.BlockSpec(memory_space=pltpu.SMEM), far, far, far, far],
+            out_specs=pl.BlockSpec(memory_space=pltpu.VMEM),
+            scratch_shapes=[
+                kept,
+                kept,
+                pltpu.VMEM(shape[1:], jnp.float32),
+                pltpu.SemaphoreType.DMA((3 * count + 1,)),
+            ],
+        )(own, gate, values, grad, taps)
+
+    arrived = near(exchange(pack(0, early)))
+    rest = near(exchange(pack(early, late)))
+    made, sums = correlate(groups, part, 0, early, arrived)
+    (made,) = correlate(groups, part, early, late, rest, arrived, made, sums)
     home = near(exchange(made))
     wide = jax.ShapeDtypeStruct(shape, jnp.bfloat16)
     local = pl.BlockSpec(memory_space=pltpu.VMEM)

time: 80 us -> 80.7 us (level)
  blocking collectives: 62.2 us -> 23.8 us
  waiting for transfers between devices: 0 us -> 26.8 us
  starting transfers between devices: 0 us -> 9.92 us
  Pallas kernels: 16.9 us -> 19.1 us
    all_to_all x2 -> x1, blocking collectives: 62.2 us -> 23.8 us  [exchange(): lax.all_to_all(array, ('dp', 'seq'), split_axis=0, concat_axis=0, tiled=T...]
    all_to_all x0 -> x2, waiting for transfers between devices: none -> 26.8 us  [exchange(): lax.all_to_all(array, ('dp', 'seq'), split_axis=0, concat_axis=0, tiled=T...]
    all_to_all x0 -> x2, starting transfers between devices: none -> 9.92 us  [exchange(): lax.all_to_all(array, ('dp', 'seq'), split_axis=0, concat_axis=0, tiled=T...]
    pallas_call x2 -> x4, Pallas kernels: 15.7 us -> 17.9 us  [the longest x2 13.8 us: correlate(): pl.pallas_call(functools.partial(correlate_body, seqs, blocks, UNROLL, pa...]
  transfers between devices with their start and end apart: 0 -> 2, of which waited for: 0 -> 2; matrix products, arithmetic and copies ran while one was open for 0% -> 0% of each run, Pallas kernels for 0% -> 14%
where the time goes in v6:
time: 80.7 us; the launch traced here: 80.3 us
  waiting for transfers between devices  26.8 us (33%)
  blocking collectives  23.8 us (29%)
  Pallas kernels  19.1 us (24%)
  starting transfers between devices  9.92 us (12%)
    all_to_all x2, waiting for transfers between devices, exchange(): lax.all_to_all(array, ('dp', 'seq'), split_axis=0, concat_axis=0, tiled=T...  26.8 us
    all_to_all x1, blocking collectives, exchange(): lax.all_to_all(array, ('dp', 'seq'), split_axis=0, concat_axis=0, tiled=T...  23.8 us
    pallas_call x2, Pallas kernels, correlate(): pl.pallas_call(functools.partial(correlate_body, seqs, blocks, UNROLL, pa...  13.8 us
    all_to_all x2, starting transfers between devices, exchange(): lax.all_to_all(array, ('dp', 'seq'), split_axis=0, concat_axis=0, tiled=T...  9.92 us
    pallas_call x2, Pallas kernels, pack(): pl.pallas_call(functools.partial(pack_body, first, count), out_shape=jax....  4.17 us
  transfers between devices with their start and end apart: 2, of which 2 were waited for; matrix products, arithmetic and copies ran while one was open for 0% of the time, Pallas kernels for 14%

profile of v6, /device:TPU:0, one launch (start us, length us, event | category | flops | bytes accessed | tf_op | source)
XLA Modules:
  0.0 80.3 jit_solution(18101331144707500832)
XLA Ops:
  0.6 2.4 %shard_map.68 = bf16[32,128,128]{2,1,0:T(8,128)(2,1)} custom-call(s32[1]{0:T(128)} %bitcast.own_ref, bf16[4,32,16,128]{3,2,1,0:T(8,128)(2,1)} %bitcast.8, bf16[4,32,16,128]{3,2,1,0:T(8,128)(2,1)} %bitcast.11, bf16[4,32,16,128]{3,2,1,0:T(8,128)(2,1)} %bitcast.16, f32[4,32,16,128]{3,2,1,0:T(8,128)} %bitcast.14), custom_call_target="tpu_custom_call" | custom-call | tf_op jit(solution)/shard_map/pallas_call | solution.py:454
  3.0 7.3 %all-to-all-start.1 = ((bf16[32,128,128]{2,1,0:T(8,128)(2,1)}), bf16[32,128,128]{2,1,0:T(8,128)(2,1)S(1)}, u32[]{:S(2)}, u32[]{:S(2)}) async-start(bf16[32,128,128]{2,1,0:T(8,128)(2,1)} %shard_map.68), calls=%async_computation.1 | async-start | bytes 2097152 | tf_op jit(solution)/shard_map/all_to_all | solution.py:433
  10.4 1.8 %shard_map.67 = bf16[32,32,128]{2,1,0:T(8,128)(2,1)} custom-call(s32[1]{0:T(128)} %bitcast.own_ref, bf16[4,32,16,128]{3,2,1,0:T(8,128)(2,1)} %bitcast.9, bf16[4,32,16,128]{3,2,1,0:T(8,128)(2,1)} %bitcast.12, bf16[4,32,16,128]{3,2,1,0:T(8,128)(2,1)} %bitcast.17, f32[4,32,16,128]{3,2,1,0:T(8,128)} %bitcast.15), custom_call_target="tpu_custom_call" | custom-call | tf_op jit(solution)/shard_map/pallas_call | solution.py:454
  12.2 25.7 %all-to-all-done.1.refs_0_.refs_1_ = bf16[32,128,128]{2,1,0:T(8,128)(2,1)S(1)} async-done(((bf16[32,128,128]{2,1,0:T(8,128)(2,1)}), bf16[32,128,128]{2,1,0:T(8,128)(2,1)S(1)}, u32[]{:S(2)}, u32[]{:S(2)}) %all-to-all-start.1) | async-done | bytes 1048608 | tf_op jit(solution)/shard_map/all_to_all | solution.py:433
  37.9 2.6 %all-to-all-start = ((bf16[32,32,128]{2,1,0:T(8,128)(2,1)}), bf16[32,32,128]{2,1,0:T(8,128)(2,1)S(1)}, u32[]{:S(2)}, u32[]{:S(2)}) async-start(bf16[32,32,128]{2,1,0:T(8,128)(2,1)} %shard_map.67), calls=%async_computation | async-start | bytes 524288 | tf_op jit(solution)/shard_map/all_to_all | solution.py:433
  40.4 9.4 %shard_map.69 = (bf16[32,48,128]{2,1,0:T(8,128)(2,1)}, bf16[24,16,128]{2,1,0:T(8,128)(2,1)}) custom-call(bf16[32,128,128]{2,1,0:T(8,128)(2,1)S(1)} %all-to-all-done.1.refs_0_.refs_1_), custom_call_target="tpu_custom_call" | custom-call | flops 12079595520 | bytes 2097152 | tf_op jit(solution)/shard_map/pallas_call | solution.py:404
  49.8 1.1 %all-to-all-done.refs_0_ = bf16[32,32,128]{2,1,0:T(8,128)(2,1)S(1)} async-done(((bf16[32,32,128]{2,1,0:T(8,128)(2,1)}), bf16[32,32,128]{2,1,0:T(8,128)(2,1)S(1)}, u32[]{:S(2)}, u32[]{:S(2)}) %all-to-all-start) | async-done | bytes 262176 | tf_op jit(solution)/shard_map/all_to_all | solution.py:433
  50.9 4.4 %shard_map.70 = bf16[32,80,128]{2,1,0:T(8,128)(2,1)} custom-call(bf16[32,32,128]{2,1,0:T(8,128)(2,1)S(1)} %all-to-all-done.refs_0_, bf16[32,128,128]{2,1,0:T(8,128)(2,1)S(1)} %all-to-all-done.1.refs_0_.refs_1_, bf16[32,48,128]{2,1,0:T(8,128)(2,1)} %get-tuple-element.8.refs_2_, bf16[24,16,128]{2,1,0:T(8,128)(2,1)} %get-tuple-element.9.refs_3_), custom_call_target="tpu_custom_call" | custom-call | flops 4026531840 | bytes 524288 | tf_op jit(solution)/shard_map/pallas_call | solution.py:404
  55.3 0.0 copy-start
  55.3 0.0 copy-start.1
  55.3 23.8 %all_to_all.15.home = bf16[32,80,128]{2,1,0:T(8,128)(2,1)S(1)} all-to-all(bf16[32,80,128]{2,1,0:T(8,128)(2,1)} %shard_map.70), channel_id=1, replica_groups=mesh['seq'=8,'dp'=4] {'dp','seq'}, dimensions={0} | all-to-all | bytes 1310720 | tf_op jit(solution)/shard_map/all_to_all | solution.py:433
  79.1 0.0 copy-done
  79.2 0.0 copy-done.1
  79.2 1.1 %shard_map.71 = (bf16[4,32,16,128]{3,2,1,0:T(8,128)(2,1)}, bf16[4,32,16,128]{3,2,1,0:T(8,128)(2,1)}, f32[32,16,128]{2,1,0:T(8,128)}) custom-call(bf16[32,80,128]{2,1,0:T(8,128)(2,1)S(1)} %all_to_all.15.home, bf16[4,32,16,128]{3,2,1,0:T(8,128)(2,1)S(1)} %bitcast.10, bf16[4,32,16,128]{3,2,1,0:T(8,128)(2,1)S(1)} %bitcast.13), custom_call_target="tpu_custom_call" | custom-call | tf_op jit(solution)/shard_map/pallas_call | solution.py:474
Async XLA Ops:
  3.0 34.8 %all-to-all-start.1 = ((bf16[32,128,128]{2,1,0:T(8,128)(2,1)}), bf16[32,128,128]{2,1,0:T(8,128)(2,1)S(1)}, u32[]{:S(2)}, u32[]{:S(2)}) async-start(bf16[32,128,128]{2,1,0:T(8,128)(2,1)} %shard_map.68), calls=%async_computation.1 | async-start | bytes 2097152 | tf_op jit(solution)/shard_map/all_to_all | solution.py:433
  37.9 13.0 %all-to-all-start = ((bf16[32,32,128]{2,1,0:T(8,128)(2,1)}), bf16[32,32,128]{2,1,0:T(8,128)(2,1)S(1)}, u32[]{:S(2)}, u32[]{:S(2)}) async-start(bf16[32,32,128]{2,1,0:T(8,128)(2,1)} %shard_map.67), calls=%async_computation | async-start | bytes 524288 | tf_op jit(solution)/shard_map/all_to_all | solution.py:433
  55.3 23.9 %copy-start = (bf16[1,2048,128]{2,1,0:T(8,128)(2,1)S(1)}, bf16[1,2048,128]{2,1,0:T(8,128)(2,1)}, u32[]{:S(2)}) copy-start(bf16[1,2048,128]{2,1,0:T(8,128)(2,1)} %param.4) | copy-start | bytes 1572868
  55.3 23.9 %copy-start.1 = (bf16[1,2048,128]{2,1,0:T(8,128)(2,1)S(1)}, bf16[1,2048,128]{2,1,0:T(8,128)(2,1)}, u32[]{:S(2)}) copy-start(bf16[1,2048,128]{2,1,0:T(8,128)(2,1)} %param.5) | copy-start | bytes 1572868

commit v7 on v5

--- a/solution.py
+++ b/solution.py
@@ -12,6 +12,7 @@
 SUBLANES = 16
 REACH = 32
 UNROLL = 8
+PIECES = 4
 ROOM = 40 * 2**20
 
 precise = lax.Precision.HIGHEST
@@ -152,37 +153,51 @@
 
 
 def pack_body(
-    groups, own_ref, gate_ref, values_ref, grad_ref, taps_ref, out_ref, gate, values, taps, sems
+    groups, pieces, own_ref, gate_ref, values_ref, grad_ref, taps_ref, out_ref,
+    gate, values, taps, made, in_sems, out_sems,
 ):
-    part = gate.shape[2]
-    loads = {}
-    loads["taps", 0] = pltpu.make_async_copy(
-        taps_ref.at[own_ref[0]], taps, sems.at[3 * groups]
-    )
-    for q in range(groups):
-        loads["gate", q] = pltpu.make_async_copy(gate_ref.at[q], gate.at[q], sems.at[2 * q])
-        loads["values", q] = pltpu.make_async_copy(
-            values_ref.at[q], values.at[q], sems.at[2 * q + 1]
+    peers, part = gate.shape[1:3]
+    size = peers // pieces
+    loads = []
+    for j in range(pieces):
+        own = pl.ds(j * size, size)
+        pairs = [
+            (gate_ref.at[:, own], gate.at[:, own]),
+            (values_ref.at[:, own], values.at[:, own]),
+            (taps_ref.at[own_ref[0], own], taps.at[own]),
+        ]
+        pairs += [
+            (grad_ref.at[q, own], made.at[own, pl.ds(q * part, part), :]) for q in range(groups)
+        ]
+        loads.append(
+            [
+                pltpu.make_async_copy(source, target, in_sems.at[j, i])
+                for i, (source, target) in enumerate(pairs)
+            ]
         )
-    for q in range(groups):
-        loads["grad", q] = pltpu.make_async_copy(
-            grad_ref.at[q], out_ref.at[:, pl.ds(q * part, part), :], sems.at[2 * groups + q]
+    for copies in loads:
+        for copy in copies:
+            copy.start()
+    sends = []
+    for j in range(pieces):
+        own = slice(j * size, (j + 1) * size)
+        for copy in loads[j][:3]:
+            copy.wait()
+        for q in range(groups):
+            product = gate[q, own].astype(jnp.float32) * values[q, own].astype(jnp.float32)
+            made[own, (groups + q) * part : (groups + q + 1) * part, :] = product.astype(jnp.bfloat16)
+        high = taps[own].astype(jnp.bfloat16)
+        made[own, 2 * groups * part : (2 * groups + 1) * part, :] = high
+        made[own, (2 * groups + 1) * part :, :] = (taps[own] - high.astype(jnp.float32)).astype(
+            jnp.bfloat16
         )
-    for copy in loads.values():
-        copy.start()
-    loads["taps", 0].wait()
-    high = taps[...].astype(jnp.bfloat16)
-    out_ref[:, 2 * groups * part : (2 * groups + 1) * part, :] = high
-    out_ref[:, (2 * groups + 1) * part :, :] = (taps[...] - high.astype(jnp.float32)).astype(
-        jnp.bfloat16
-    )
-    for q in range(groups):
-        loads["gate", q].wait()
-        loads["values", q].wait()
-        product = gate[q].astype(jnp.float32) * values[q].astype(jnp.float32)
-        out_ref[:, (groups + q) * part : (groups + q + 1) * part, :] = product.astype(jnp.bfloat16)
-    for q in range(groups):
-        loads["grad", q].wait()
+        for copy in loads[j][3:]:
+            copy.wait()
+        rows = pl.ds(j * size, size)
+        sends.append(pltpu.make_async_copy(made.at[rows], out_ref.at[rows], out_sems.at[j]))
+        sends[-1].start()
+    for copy in sends:
+        copy.wait()
 
 
 def correlate_body(seqs, blocks, unroll, in_ref, out_ref, gs, ms, fs, cs, rs, pads, hs0, ts0, tn0, hs1, ts1, tn1):
@@ -398,19 +413,22 @@
     shape = (groups, peers, part, LANES)
     gate, values, grad = (array.reshape(shape) for array in (gate_in, values_in, out_grad))
     taps = filter_taps.reshape(shape)
+    pieces = math.gcd(peers, PIECES)
     own = lax.axis_index("dp").astype(jnp.int32).reshape(1)
     far = pl.BlockSpec(memory_space=pl.ANY)
     half = pltpu.VMEM(shape, jnp.bfloat16)
     packed = pl.pallas_call(
-        functools.partial(pack_body, groups),
+        functools.partial(pack_body, groups, pieces),
         out_shape=jax.ShapeDtypeStruct((peers, (2 * groups + 2) * part, LANES), jnp.bfloat16),
         in_specs=[pl.BlockSpec(memory_space=pltpu.SMEM), far, far, far, far],
-        out_specs=pl.BlockSpec(memory_space=pltpu.VMEM),
+        out_specs=far,
         scratch_shapes=[
             half,
             half,
             pltpu.VMEM(shape[1:], jnp.float32),
-            pltpu.SemaphoreType.DMA((3 * groups + 1,)),
+            pltpu.VMEM((peers, (2 * groups + 2) * part, LANES), jnp.bfloat16),
+            pltpu.SemaphoreType.DMA((pieces, groups + 3)),
+            pltpu.SemaphoreType.DMA((pieces,)),
         ],
     )(own, gate, values, grad, taps)
     near = functools.partial(pltpu.with_memory_space_constraint, memory_space=pltpu.VMEM)

time: 80 us -> 79.9 us (level)
  no operation moved by 1% of the time
where the time goes in v7:
time: 79.9 us; the launch traced here: 79.6 us
  blocking collectives  62.2 us (78%)
  Pallas kernels  16.8 us (21%)
    all_to_all x2, blocking collectives, exchange(): lax.all_to_all(array, ('dp', 'seq'), split_axis=0, concat_axis=0, tiled=T...  62.2 us
    pallas_call x1, Pallas kernels, correlate(): pl.pallas_call(functools.partial(correlate_body, seqs, blocks, UNROLL), o...  13.1 us
    pallas_call x1, Pallas kernels, direct_shards(): pl.pallas_call(functools.partial(pack_body, groups, pieces), out_shape=ja...  2.55 us

profile of v7, /device:TPU:0, one launch (start us, length us, event | category | flops | bytes accessed | tf_op | source)
XLA Modules:
  0.0 79.6 jit_solution(17095603164131793588)
XLA Ops:
  0.6 2.5 %shard_map.67 = bf16[32,160,128]{2,1,0:T(8,128)(2,1)} custom-call(s32[1]{0:T(128)} %bitcast.own_ref, bf16[4,32,16,128]{3,2,1,0:T(8,128)(2,1)} %bitcast.8, bf16[4,32,16,128]{3,2,1,0:T(8,128)(2,1)} %bitcast.10, bf16[4,32,16,128]{3,2,1,0:T(8,128)(2,1)} %bitcast.13, f32[4,32,16,128]{3,2,1,0:T(8,128)} %bitcast.12), custom_call_target="tpu_custom_call" | custom-call | tf_op jit(solution)/shard_map/pallas_call | solution.py:420
  3.2 40.4 %all_to_all.10.in_ref = bf16[32,160,128]{2,1,0:T(8,128)(2,1)S(1)} all-to-all(bf16[32,160,128]{2,1,0:T(8,128)(2,1)} %shard_map.67), channel_id=1, replica_groups=mesh['seq'=8,'dp'=4] {'dp','seq'}, dimensions={0} | all-to-all | bytes 2621440 | tf_op jit(solution)/shard_map/all_to_all | solution.py:405
  43.6 13.1 %shard_map.68 = bf16[32,80,128]{2,1,0:T(8,128)(2,1)} custom-call(bf16[32,160,128]{2,1,0:T(8,128)(2,1)S(1)} %all_to_all.10.in_ref), custom_call_target="tpu_custom_call" | custom-call | flops 1610612736 | bytes 2621440 | tf_op jit(solution)/shard_map/pallas_call | solution.py:379
  56.7 0.0 copy-start
  56.7 0.0 copy-start.1
  56.7 21.8 %all_to_all.11.home = bf16[32,80,128]{2,1,0:T(8,128)(2,1)S(1)} all-to-all(bf16[32,80,128]{2,1,0:T(8,128)(2,1)} %shard_map.68), channel_id=1, replica_groups=mesh['seq'=8,'dp'=4] {'dp','seq'}, dimensions={0} | all-to-all | bytes 1310720 | tf_op jit(solution)/shard_map/all_to_all | solution.py:405
  78.5 0.0 copy-done
  78.5 0.0 copy-done.1
  78.5 1.1 %shard_map.69 = (bf16[4,32,16,128]{3,2,1,0:T(8,128)(2,1)}, bf16[4,32,16,128]{3,2,1,0:T(8,128)(2,1)}, f32[32,16,128]{2,1,0:T(8,128)}) custom-call(bf16[32,80,128]{2,1,0:T(8,128)(2,1)S(1)} %all_to_all.11.home, bf16[4,32,16,128]{3,2,1,0:T(8,128)(2,1)S(1)} %bitcast.9, bf16[4,32,16,128]{3,2,1,0:T(8,128)(2,1)S(1)} %bitcast.11), custom_call_target="tpu_custom_call" | custom-call | tf_op jit(solution)/shard_map/pallas_call | solution.py:440
Async XLA Ops:
  56.7 21.8 %copy-start = (bf16[1,2048,128]{2,1,0:T(8,128)(2,1)S(1)}, bf16[1,2048,128]{2,1,0:T(8,128)(2,1)}, u32[]{:S(2)}) copy-start(bf16[1,2048,128]{2,1,0:T(8,128)(2,1)} %param.4) | copy-start | bytes 1572868
  56.7 21.8 %copy-start.1 = (bf16[1,2048,128]{2,1,0:T(8,128)(2,1)S(1)}, bf16[1,2048,128]{2,1,0:T(8,128)(2,1)}, u32[]{:S(2)}) copy-start(bf16[1,2048,128]{2,1,0:T(8,128)(2,1)} %param.5) | copy-start | bytes 1572868

commit v8 on v7

--- a/solution.py
+++ b/solution.py
@@ -11,7 +11,6 @@
 LANES = 128
 SUBLANES = 16
 REACH = 32
-UNROLL = 8
 PIECES = 4
 ROOM = 40 * 2**20
 
@@ -200,7 +199,7 @@
         copy.wait()
 
 
-def correlate_body(seqs, blocks, unroll, in_ref, out_ref, gs, ms, fs, cs, rs, pads, hs0, ts0, tn0, hs1, ts1, tn1):
+def correlate_body(seqs, blocks, unroll, in_ref, out_ref, gs, ms, fs, cs, rs, pads, hs0, ts0, tn0, hs1, ts1, tn1, stage, sems):
     peers = seqs * blocks
     part = in_ref.shape[1] // (2 * seqs + 2)
     held = seqs * part
@@ -341,15 +340,29 @@
         turn_over(after, tn0)
         multiply(2 * i + 1, hs1, ts1, tn1)
         build(after, hs0, ts0)
+        for p in range(peers):
+            mine = cs[pl.ds(pl.multiple_of(p * held + i * part, part), part), :]
+            stage[i, p] = mine.astype(jnp.bfloat16)
+        pltpu.make_async_copy(
+            stage.at[i], out_ref.at[:, pl.ds(pl.multiple_of(i * part, part), part), :], sems.at[i]
+        ).start()
         return carry
 
     lax.fori_loop(0, total // 2, twice, 0)
-    out_ref[:, :held, :] = cs[...].reshape(peers, held, LANES).astype(jnp.bfloat16)
     for q in range(seqs):
-        for s in range(blocks):
-            out_ref[q * blocks + s, held:, :] = rs[pl.ds(s * held + q * part, part), :].astype(
+        for b in range(blocks):
+            stage[seqs, q * blocks + b] = rs[pl.ds(b * held + q * part, part), :].astype(
                 jnp.bfloat16
             )
+    sends = [
+        pltpu.make_async_copy(
+            stage.at[q], out_ref.at[:, pl.ds(q * part, part), :], sems.at[q]
+        )
+        for q in range(seqs + 1)
+    ]
+    sends[seqs].start()
+    for copy in sends:
+        copy.wait()
 
 
 def unpack_body(
@@ -377,23 +390,25 @@
     held = seqs * part
     whole = pl.BlockSpec(memory_space=pltpu.VMEM)
     return pl.pallas_call(
-        functools.partial(correlate_body, seqs, blocks, UNROLL),
+        functools.partial(correlate_body, seqs, blocks, (part // 2)),
         out_shape=jax.ShapeDtypeStruct((peers, held + part, LANES), jnp.bfloat16),
         in_specs=[whole],
-        out_specs=whole,
+        out_specs=pl.BlockSpec(memory_space=pl.ANY),
         scratch_shapes=[
             pltpu.VMEM((peers * held, LANES), jnp.float32),
             pltpu.VMEM((peers * held, LANES), jnp.float32),
             pltpu.VMEM((blocks * held, LANES), jnp.float32),
             pltpu.VMEM((peers * held, LANES), jnp.float32),
             pltpu.VMEM((blocks * held, LANES), jnp.float32),
-            pltpu.VMEM((UNROLL * (LANES // REACH) * 2 * peers, LANES), jnp.float32),
+            pltpu.VMEM(((part // 2) * (LANES // REACH) * 2 * peers, LANES), jnp.float32),
             *[
-                pltpu.VMEM((UNROLL, blocks, LANES // REACH * peers, LANES), jnp.bfloat16),
-                pltpu.VMEM((UNROLL, blocks, 2 * REACH, LANES), jnp.bfloat16),
-                pltpu.VMEM((UNROLL, REACH, LANES // REACH * peers), jnp.bfloat16),
+                pltpu.VMEM(((part // 2), blocks, LANES // REACH * peers, LANES), jnp.bfloat16),
+                pltpu.VMEM(((part // 2), blocks, 2 * REACH, LANES), jnp.bfloat16),
+                pltpu.VMEM(((part // 2), REACH, LANES // REACH * peers), jnp.bfloat16),
             ]
             * 2,
+            pltpu.VMEM((seqs + 1, peers, part, LANES), jnp.bfloat16),
+            pltpu.SemaphoreType.DMA((seqs + 1,)),
         ],
         cost_estimate=pl.CostEstimate(
             flops=6 * held * LANES * blocks * LANES * peers, bytes_accessed=4 * arrived.size, transcendentals=0

time: 79.9 us -> 80 us (level)
  no operation moved by 1% of the time
where the time goes in v8:
time: 80 us; the launch traced here: 79.7 us
  blocking collectives  62.2 us (78%)
  Pallas kernels  16.8 us (21%)
    all_to_all x2, blocking collectives, exchange(): lax.all_to_all(array, ('dp', 'seq'), split_axis=0, concat_axis=0, tiled=T...  62.2 us
    pallas_call x1, Pallas kernels, correlate(): pl.pallas_call(functools.partial(correlate_body, seqs, blocks, part // 2)...  13.1 us
    pallas_call x1, Pallas kernels, direct_shards(): pl.pallas_call(functools.partial(pack_body, groups, pieces), out_shape=ja...  2.55 us

profile of v8, /device:TPU:0, one launch (start us, length us, event | category | flops | bytes accessed | tf_op | source)
XLA Modules:
  0.0 79.7 jit_solution(7774170133084881210)
XLA Ops:
  0.6 2.5 %shard_map.67 = bf16[32,160,128]{2,1,0:T(8,128)(2,1)} custom-call(s32[1]{0:T(128)} %bitcast.own_ref, bf16[4,32,16,128]{3,2,1,0:T(8,128)(2,1)} %bitcast.8, bf16[4,32,16,128]{3,2,1,0:T(8,128)(2,1)} %bitcast.10, bf16[4,32,16,128]{3,2,1,0:T(8,128)(2,1)} %bitcast.13, f32[4,32,16,128]{3,2,1,0:T(8,128)} %bitcast.12), custom_call_target="tpu_custom_call" | custom-call | tf_op jit(solution)/shard_map/pallas_call | solution.py:435
  3.2 40.4 %all_to_all.10.in_ref = bf16[32,160,128]{2,1,0:T(8,128)(2,1)S(1)} all-to-all(bf16[32,160,128]{2,1,0:T(8,128)(2,1)} %shard_map.67), channel_id=1, replica_groups=mesh['seq'=8,'dp'=4] {'dp','seq'}, dimensions={0} | all-to-all | bytes 2621440 | tf_op jit(solution)/shard_map/all_to_all | solution.py:420
  43.6 13.1 %shard_map.68 = bf16[32,80,128]{2,1,0:T(8,128)(2,1)} custom-call(bf16[32,160,128]{2,1,0:T(8,128)(2,1)S(1)} %all_to_all.10.in_ref), custom_call_target="tpu_custom_call" | custom-call | flops 1610612736 | bytes 2621440 | tf_op jit(solution)/shard_map/pallas_call | solution.py:392
  56.7 0.0 copy-start
  56.7 0.0 copy-start.1
  56.7 21.8 %all_to_all.11.home = bf16[32,80,128]{2,1,0:T(8,128)(2,1)S(1)} all-to-all(bf16[32,80,128]{2,1,0:T(8,128)(2,1)} %shard_map.68), channel_id=1, replica_groups=mesh['seq'=8,'dp'=4] {'dp','seq'}, dimensions={0} | all-to-all | bytes 1310720 | tf_op jit(solution)/shard_map/all_to_all | solution.py:420
  78.5 0.0 copy-done
  78.5 0.0 copy-done.1
  78.5 1.1 %shard_map.69 = (bf16[4,32,16,128]{3,2,1,0:T(8,128)(2,1)}, bf16[4,32,16,128]{3,2,1,0:T(8,128)(2,1)}, f32[32,16,128]{2,1,0:T(8,128)}) custom-call(bf16[32,80,128]{2,1,0:T(8,128)(2,1)S(1)} %all_to_all.11.home, bf16[4,32,16,128]{3,2,1,0:T(8,128)(2,1)S(1)} %bitcast.9, bf16[4,32,16,128]{3,2,1,0:T(8,128)(2,1)S(1)} %bitcast.11), custom_call_target="tpu_custom_call" | custom-call | tf_op jit(solution)/shard_map/pallas_call | solution.py:455
Async XLA Ops:
  56.7 21.8 %copy-start = (bf16[1,2048,128]{2,1,0:T(8,128)(2,1)S(1)}, bf16[1,2048,128]{2,1,0:T(8,128)(2,1)}, u32[]{:S(2)}) copy-start(bf16[1,2048,128]{2,1,0:T(8,128)(2,1)} %param.4) | copy-start | bytes 1572868
  56.7 21.8 %copy-start.1 = (bf16[1,2048,128]{2,1,0:T(8,128)(2,1)S(1)}, bf16[1,2048,128]{2,1,0:T(8,128)(2,1)}, u32[]{:S(2)}) copy-start(bf16[1,2048,128]{2,1,0:T(8,128)(2,1)} %param.5) | copy-start | bytes 1572868
